TPU v7x, 256 devices: a whole 4x4x8 slice. The times are simulated.
256 devices in a mesh: tile: 32 (over z, y_hi, core), cam: 8 (over y_lo, x).
Axes of the slice: x: 4, y: 4 (y_hi: 2, y_lo: 2; y = y_hi * 2 + y_lo), z: 8, core: 2. Of those that a mesh axis runs over, the one named last changes fastest.
Arguments:
- features: bfloat16 [6144, 256], P(('tile', 'cam')), may hold values from -6 to 6
- value_weight: bfloat16 [256, 256], replicated, may hold values from -0.375 to 0.375
- output_weight: bfloat16 [256, 256], replicated, may hold values from -0.375 to 0.375
- hit_list: int32 [32, 2], P('tile'), may hold values from 0 to 5, as said below
- sample_index: int32 [16384, 2, 64], P('tile'), may hold values from 0 to 1023, as said below
- attention: bfloat16 [16384, 64], P('tile'), may hold values from 0.0099487305 to 1
- validity: int32 [16384, 2], P('tile'), may hold values from 0 to 1, as said below
Outputs:
- projected: bfloat16 [16384, 256], P(('tile', 'cam'))
Inputs may be any that keep to these rules, and one draw needn't show every extreme that they name: `hit_list`: camera numbers 0 to 5; where a tile sees one camera its two entries are equal. `validity`: where a tile's two hit_list entries are equal, the second column is 0 for every query of that tile. `sample_index`: for one query, slot and head, the 8 entries h * 8 to h * 8 + 7 all differ.
All inputs are finite; a program needn't handle non-finite values.
Results may differ from a plain program's by a relative error of at most 0.0058.
Values may be sent and summed in bfloat16 or wider, within the bound.
No kernel may reach another device: no remote copies, remote signals or barrier semaphores. Data moves between devices by JAX's collectives and lax.ppermute only.
A program may use at most 64 MiB of HBM per device.

v0:
```python
import jax
import jax.numpy as jnp
from jax import lax
from jax.sharding import PartitionSpec as P

D = 256
H = 8
K = 8
HITS = 2
CAM_ROWS = 1024


lane_width = 128
block_limit = 1 << 22


def sent_to_all(x, axis):
    length = lax.axis_size(axis)
    return lax.all_to_all(jnp.broadcast_to(x[None], (length, *x.shape)), axis, 0, 0, tiled=True)


def laid_out(pieces, dim):
    lengths = list(pieces.shape[1:])
    lengths[dim] *= pieces.shape[0]
    return jnp.moveaxis(pieces, 0, dim).reshape(lengths)


def gather_directly(x, axis, dim):
    pieces = sent_to_all(x, axis)
    return laid_out(pieces, dim)


def in_blocks(x, dim, length):
    lengths = x.shape
    pieces = x.reshape(*lengths[:dim], length, lengths[dim] // length, *lengths[dim + 1 :])
    return jnp.moveaxis(pieces, dim, 0)


def sum_at_owner(x, axis, dim):
    pieces = in_blocks(x, dim, lax.axis_size(axis))
    arrived = lax.all_to_all(pieces, axis, split_axis=0, concat_axis=0, tiled=True)
    return arrived.sum(axis=0)


def request_table(hit_row, sample_index, attention, validity):
    queries = sample_index.shape[0]
    targets = hit_row[None, :, None] * CAM_ROWS + sample_index
    targets = (
        targets.reshape(queries, HITS, H, K).transpose(0, 2, 1, 3).reshape(queries, H, HITS * K)
    )
    hit_count = jnp.sum(validity, axis=1)
    inverse = 1.0 / jnp.maximum(hit_count, 1).astype(jnp.float32)
    weights = (
        attention.astype(jnp.float32).reshape(queries, 1, H, K)
        * validity.astype(jnp.float32)[:, :, None, None]
    )
    weights = weights * inverse[:, None, None, None]
    weights = weights.transpose(0, 2, 1, 3).reshape(queries, H, HITS * K).astype(jnp.bfloat16)
    return (targets, weights)


def sample_piece(running, section, first_row, positions, weights):
    row_count, width = section.shape
    queries = positions.shape[0]
    offset = first_row % lane_width
    groups = (row_count + lane_width - 1) // lane_width + 1
    buffer = jnp.zeros((groups * lane_width, width), section.dtype)
    buffer = lax.dynamic_update_slice_in_dim(buffer, section, offset, 0)
    high_part = positions // lane_width
    low_hot = ((positions % lane_width)[..., None] == jnp.arange(lane_width)).astype(jnp.bfloat16)
    per_block = max(1, block_limit // (queries * H * lane_width))
    block_groups = 1
    for candidate in range(min(groups, per_block), 0, -1):
        block_groups = candidate
        break

    def one_block(block_id, summed):
        first_group = block_id * block_groups
        high_hot = jnp.where(
            high_part[..., None] - first_group == jnp.arange(block_groups),
            weights[..., None],
            jnp.zeros((), jnp.bfloat16),
        )
        mixing = jnp.einsum(
            "qhsa,qhsb->qhab", high_hot, low_hot, preferred_element_type=jnp.float32
        )
        mixing = mixing.reshape(queries, H, block_groups * lane_width).astype(jnp.bfloat16)
        block_values = buffer
        block_values = block_values.reshape(block_groups * lane_width, H, width // H)
        return summed + jnp.einsum(
            "qhr,rhd->qhd", mixing, block_values, preferred_element_type=jnp.float32
        )

    return lax.fori_loop(0, groups // block_groups, one_block, running)


def body(features, value_weight, output_weight, hit_list, sample_index, attention, validity):
    values = jnp.dot(features, value_weight, preferred_element_type=jnp.float32).astype(
        jnp.bfloat16
    )
    shard_rows = features.shape[0]
    cam_total = lax.axis_size("cam")
    cam_place = lax.axis_index("cam")
    tile_queries = sample_index.shape[0]
    targets, weights = request_table(hit_list[0], sample_index, attention, validity)
    owner = targets // shard_rows
    positions = jnp.where(
        owner % cam_total == cam_place, owner // cam_total * shard_rows + targets % shard_rows, -1
    )
    empty = jnp.zeros((tile_queries, H, D // H), jnp.float32)
    partial_value = sample_piece(
        empty, gather_directly(values, "tile", 0), jnp.int32(0), positions, weights
    )
    sampled = sum_at_owner(partial_value.reshape(tile_queries, D), "cam", 0)
    attended = sampled.astype(jnp.bfloat16)
    return jnp.dot(attended, output_weight, preferred_element_type=jnp.float32).astype(jnp.bfloat16)


def solution(mesh):
    in_specs = (
        P(("tile", "cam"), None),
        P(),
        P(),
        P("tile", None),
        P("tile", None, None),
        P("tile", None),
        P("tile", None),
    )
    out_specs = P(("tile", "cam"), None)
    return jax.shard_map(body, mesh=mesh, in_specs=in_specs, out_specs=out_specs, check_vma=False)
```

profile of v0, /device:TPU:16, one launch (start us, length us, event | category | flops | bytes accessed | tf_op | source)
XLA Modules:
  0.0 76.4 jit_solution(12717795853007933718)
XLA Ops:
  0.0 0.0 copy-start
  0.0 1.1 %convolution_convert_fusion.1 = bf16[24,256]{1,0:T(8,128)(2,1)S(1)} fusion(bf16[24,256]{1,0:T(8,128)(2,1)} %param.7, bf16[256,256]{1,0:T(8,128)(2,1)} %param.8), kind=kOutput, calls=%fused_computation.13 | convolution fusion | flops 3151872 | bytes 155648 | tf_op jit(solution)/shard_map/dot_general | solution.py:98
  1.1 0.8 %broadcast_in_dim.36 = bf16[32,24,256]{2,1,0:T(8,128)(2,1)} broadcast(bf16[24,256]{1,0:T(8,128)(2,1)S(1)} %convolution_convert_fusion.1), dimensions={1,2} | broadcast | bytes 405504 | tf_op jit(solution)/shard_map/broadcast_in_dim | solution.py:19
  1.9 11.6 %all-to-all-start = ((bf16[32,24,256]{2,1,0:T(8,128)(2,1)}), bf16[32,24,256]{2,1,0:T(8,128)(2,1)S(1)}, u32[]{:S(2)}, u32[]{:S(2)}) async-start(bf16[32,24,256]{2,1,0:T(8,128)(2,1)} %broadcast_in_dim.36), calls=%async_computation | async-start | bytes 786432 | tf_op jit(solution)/shard_map/all_to_all | solution.py:19
  13.5 0.7 multiply_bitcast_fusion
  14.2 1.1 %remainder_bitcast_fusion = (s32[512,8,2,8]{0,3,1,2:T(8,128)S(1)}, s32[512,8,2,8]{0,3,1,2:T(8,128)S(1)}) fusion(s32[512,2,64]{0,2,1:T(8,128)} %param.11, s32[2]{0:T(128)S(1)} %multiply_bitcast_fusion), kind=kLoop, calls=%fused_computation.38 | loop fusion | flops 196608 | bytes 786440 | tf_op jit(solution)/shard_map/jit(floor_divide)/rem | solution.py:106
  15.3 1.6 %add_select_fusion.1 = (s32[512,8,16]{0,2,1:T(8,128)S(1)}, s32[512,8,16]{0,2,1:T(8,128)S(1)}) fusion(s32[]{:T(128)S(6)} %axis_index.12, s32[512,8,2,8]{0,3,1,2:T(8,128)S(1)} %get-tuple-element.20, s32[512,8,2,8]{0,3,1,2:T(8,128)S(1)} %get-tuple-element.19, s32[512,2,64]{0,2,1:T(8,128)} %param.11, s32[2]{0:T(128)S(1)} %multiply_bitcast_fusion), kind=kLoop, calls=%fused_computation.15 | loop fusion | flops 3211264 | bytes 1310732 | tf_op jit(solution)/shard_map/jit(floor_divide)/jit(_where)/select_n | solution.py:69
  16.9 0.1 add_select_fusion
  17.0 0.7 copy.31
  17.7 2.0 %copy.29 = s32[512,8,16]{2,1,0:T(8,128)} copy(s32[512,8,16]{0,2,1:T(8,128)S(1)} %get-tuple-element.17) | data formatting | bytes 524288 | tf_op jit(solution)/shard_map/jit(floor_divide)/jit(_where)/select_n | solution.py:69
  19.7 0.0 copy-done.2
  19.8 0.0 copy-done.1
  19.8 1.7 %copy.30 = bf16[512,8,16]{2,1,0:T(8,128)(2,1)} copy(bf16[512,8,16]{0,2,1:T(8,128)(2,1)S(1)} %fusion.20) | data formatting | bytes 262144 | tf_op jit(solution)/shard_map/convert_element_type | solution.py:58
  21.5 17.2 %fusion.7 = bf16[512,8,7,128]{3,2,1,0:T(8,128)(2,1)} fusion(s32[512,8,16]{2,1,0:T(8,128)S(1)} %copy.31, s32[512,8,16]{2,1,0:T(8,128)} %copy.29, bf16[512,8,16]{2,1,0:T(8,128)(2,1)} %copy.30), kind=kOutput, calls=%fused_computation.8 | convolution fusion | flops 130416640 | bytes 7995392 | tf_op jit(solution)/shard_map/while/body/eval_jaxpr/qhsa,qhsb->qhab/dot_general | solution.py:84
  38.7 15.2 %convert_element_type.40 = bf16[512,8,896]{2,1,0:T(8,128)(2,1)} reshape(bf16[512,8,7,128]{3,2,1,0:T(8,128)(2,1)} %fusion.7) | data formatting | bytes 14680064 | tf_op jit(solution)/shard_map/while/body/eval_jaxpr/convert_element_type | solution.py:87
  53.9 0.0 all-to-all-done
  53.9 0.2 copy.36
  54.2 5.4 %fusion.12 = f32[512,8,32]{0,2,1:T(8,128)S(1)} fusion(bf16[896,8,32]{0,2,1:T(8,128)(2,1)S(1)} %bitcast.60, bf16[512,8,896]{2,1,0:T(8,128)(2,1)} %convert_element_type.40), kind=kOutput, calls=%fused_computation.11 | convolution fusion | flops 234881024 | bytes 8323072 | tf_op jit(solution)/shard_map/while/body/eval_jaxpr/qhr,rhd->qhd/dot_general | solution.py:90
  59.6 0.2 reshape_reshape.3
  59.8 0.4 copy.33
  60.2 15.2 %all_to_all.10 = f32[8,64,256]{2,1,0:T(8,128)S(1)} all-to-all(f32[8,64,256]{2,1,0:T(8,128)S(1)} %copy.33), channel_id=1, replica_groups=mesh['tile'=32,'cam'=8] {'cam'}, dimensions={0} | all-to-all | bytes 1048576 | tf_op jit(solution)/shard_map/all_to_all | solution.py:41
  75.5 0.1 copy.35
  75.6 0.0 copy-done
  75.6 0.8 %convolution_convert_fusion = bf16[64,256]{1,0:T(8,128)(2,1)} fusion(bf16[256,256]{1,0:T(8,128)(2,1)S(1)} %copy-done, bf16[64,256]{0,1:T(8,128)(2,1)S(1)} %copy.35), kind=kOutput, calls=%fused_computation.12 | convolution fusion | flops 8404992 | bytes 196608 | tf_op jit(solution)/shard_map/dot_general | solution.py:116
  (9 shorter events, 0.1 us)
Async XLA Ops:
  0.0 75.6 %copy-start = (bf16[256,256]{1,0:T(8,128)(2,1)S(1)}, bf16[256,256]{1,0:T(8,128)(2,1)}, u32[]{:S(2)}) copy-start(bf16[256,256]{1,0:T(8,128)(2,1)} %param.9) | copy-start | bytes 393220
  0.0 19.7 %copy-start.2 = (s32[512,2]{0,1:T(2,128)S(1)}, s32[512,2]{0,1:T(2,128)}, u32[]{:S(2)}) copy-start(s32[512,2]{0,1:T(2,128)} %param.13) | copy-start | bytes 12292
  0.0 19.8 %copy-start.1 = (bf16[512,64]{0,1:T(8,128)(2,1)S(1)}, bf16[512,64]{0,1:T(8,128)(2,1)}, u32[]{:S(2)}) copy-start(bf16[512,64]{0,1:T(8,128)(2,1)} %param.12) | copy-start | bytes 196612
  1.9 52.0 %all-to-all-start = ((bf16[32,24,256]{2,1,0:T(8,128)(2,1)}), bf16[32,24,256]{2,1,0:T(8,128)(2,1)S(1)}, u32[]{:S(2)}, u32[]{:S(2)}) async-start(bf16[32,24,256]{2,1,0:T(8,128)(2,1)} %broadcast_in_dim.36), calls=%async_computation | async-start | bytes 786432 | tf_op jit(solution)/shard_map/all_to_all | solution.py:19
where the time goes:
time: 77.2 us; the launch traced here: 76.4 us
  matrix products  24.5 us (32%)
  local copies, waits for them, and re-layouts  21.4 us (28%)
  blocking collectives  15.2 us (20%)
  starting transfers between devices  11.6 us (15%)
  other arithmetic  3.57 us (5%)
    dot_general x1, matrix products, one_block(): jnp.einsum('qhsa,qhsb->qhab', high_hot, low_hot, preferred_element_type=j...  17.2 us
    all_to_all x1, blocking collectives, sum_at_owner(): lax.all_to_all(pieces, axis, split_axis=0, concat_axis=0, tiled=True)  15.2 us
    convert_element_type x1, local copies, waits for them, and re-layouts, one_block(): mixing.reshape(queries, H, block_groups * lane_width).astype(jnp.bfloat16)  15.2 us
    all_to_all x1, starting transfers between devices, sent_to_all(): lax.all_to_all(jnp.broadcast_to(x[None], (length, *x.shape)), axis, 0, 0,...  11.6 us
    dot_general x1, matrix products, one_block(): jnp.einsum('qhr,rhd->qhd', mixing, block_values, preferred_element_type=j...  5.44 us
    select_n x1, local copies, waits for them, and re-layouts, sample_piece(): high_part = positions // lane_width  1.99 us
    convert_element_type x1, local copies, waits for them, and re-layouts, request_table(): weights.transpose(0, 2, 1, 3).reshape(queries, H, HITS * K)  1.68 us
    select_n x1, other arithmetic, sample_piece(): high_part = positions // lane_width  1.58 us
  transfers between devices with their start and end apart: 1, of which 0 were waited for; matrix products, arithmetic and copies ran while one was open for 53% of the time, Pallas kernels for 0%

commit v1 on v0

v1 whole, which is shorter than its diff:
```python
import jax
import jax.numpy as jnp
from jax import lax
from jax.experimental import pallas as pl
from jax.experimental.pallas import tpu as pltpu
from jax.sharding import Mesh, PartitionSpec as P

D = 256
H = 8
K = 8
HITS = 2
CAM_ROWS = 1024
Q = 512
CAM_DEVICES = 8

BLOCK = 24
STRIPE = CAM_DEVICES * BLOCK
WINDOW = 3 * BLOCK
CHUNK = 16
LANES = H * CHUNK
CHUNKS = 2 * HITS * WINDOW // CHUNK
Q_STEP = 32

whole = pl.BlockSpec(memory_space=pltpu.VMEM)
scalars = pl.BlockSpec(memory_space=pltpu.SMEM)


def slot_chunks(slot):
    found = []
    for half in range(2):
        first = (half * HITS + slot) * WINDOW
        found += range(first // CHUNK, (first + WINDOW - 1) // CHUNK + 1)
    return found


def mix_kernel(place_ref, hit_ref, index_ref, attention_ref, validity_ref, mix_ref, row_ref, weight_ref):
    core, cam = place_ref[0], place_ref[1]
    hit_count = validity_ref[0:1, :] + validity_ref[1:2, :]
    inverse = 1.0 / jnp.maximum(hit_count, 1).astype(jnp.float32)
    attention = attention_ref[...].astype(jnp.float32)
    rows, weights = [], []
    for slot in range(HITS):
        camera = hit_ref[0, slot]
        stripe = (camera * 16) // 3
        shifted = index_ref[slot] + (camera * CAM_ROWS - stripe * STRIPE)
        step = (shifted * 683) >> 17
        within = shifted - step * STRIPE
        owner = (within * 171) >> 12
        row = within - owner * BLOCK + (step >> 1) * BLOCK
        other = ((step + stripe) & 1) != core
        row = jnp.where(other, row + HITS * WINDOW, row)
        row = jnp.where(owner == cam, row, -2 * CHUNK)
        rows.append(row.astype(jnp.float32))
        weights.append(attention * validity_ref[slot : slot + 1, :].astype(jnp.float32) * inverse)
    rows = jnp.concatenate(rows, axis=0).T.astype(jnp.bfloat16)
    weights = jnp.concatenate(weights, axis=0).T.astype(jnp.bfloat16)
    source = lax.broadcasted_iota(jnp.int32, (HITS * H * K, LANES), 0)
    lane = lax.broadcasted_iota(jnp.int32, (HITS * H * K, LANES), 1)
    for slot in range(HITS):
        for k in range(K):
            spread = (source == slot * H * K + (lane // CHUNK) * K + k).astype(jnp.bfloat16)
            row_ref[slot * K + k] = jnp.dot(rows, spread, preferred_element_type=jnp.float32)
            weight_ref[slot * K + k] = jnp.dot(weights, spread, preferred_element_type=jnp.float32)

    local = lax.broadcasted_iota(jnp.int32, (1, LANES), 1) % CHUNK

    @pl.loop(0, Q // Q_STEP)
    def _(step):
        part = pl.ds(pl.multiple_of(step * Q_STEP, Q_STEP), Q_STEP)
        sums = {}
        for slot in range(HITS):
            picked = [row_ref[slot * K + k, part, :] for k in range(K)]
            scale = [weight_ref[slot * K + k, part, :] for k in range(K)]
            for chunk in slot_chunks(slot):
                target = (local + (chunk * CHUNK - slot * WINDOW)).astype(jnp.float32)
                total = sums.get(chunk)
                if total is None:
                    total = jnp.zeros((Q_STEP, LANES), jnp.float32)
                for k in range(K):
                    total = jnp.where(picked[k] == target, scale[k], total)
                sums[chunk] = total
        for chunk, total in sums.items():
            mix_ref[part, chunk * LANES : (chunk + 1) * LANES] = total.astype(jnp.bfloat16)


def build_mix(place, hit_list, index, attention, validity):
    return pl.pallas_call(
        mix_kernel,
        out_shape=jax.ShapeDtypeStruct((Q, CHUNKS * LANES), jnp.bfloat16),
        in_specs=[scalars, scalars, whole, whole, whole],
        out_specs=whole,
        scratch_shapes=[
            pltpu.VMEM((HITS * K, Q, LANES), jnp.float32),
            pltpu.VMEM((HITS * K, Q, LANES), jnp.float32),
        ],
        compiler_params=pltpu.CompilerParams(vmem_limit_bytes=24 << 20),
        cost_estimate=pl.CostEstimate(flops=1 << 29, bytes_accessed=4 << 20, transcendentals=0),
        name="build_mix",
    )(place, hit_list, index, attention, validity)


def sample_kernel(place_ref, hit_ref, mine_ref, other_ref, weight_ref, mix_ref, out_ref):
    core = place_ref[0]
    windows = []
    for ref, parity in ((mine_ref, core), (other_ref, 1 - core)):
        for slot in range(HITS):
            stripe = (hit_ref[0, slot] * 16) // 3
            first = ((stripe + 1 - parity) // 2) * BLOCK
            windows.append(ref[pl.ds(pl.multiple_of(first, 8), WINDOW), :])
    features = jnp.concatenate(windows, axis=0)
    values = jnp.dot(features, weight_ref[...], preferred_element_type=jnp.float32)
    head_of_row = lax.broadcasted_iota(jnp.int32, (LANES, D), 0) // CHUNK
    head_of_column = lax.broadcasted_iota(jnp.int32, (LANES, D), 1) // (D // H)
    same_head = head_of_row == head_of_column
    total = jnp.zeros((Q, D), jnp.float32)
    for pair in range(CHUNKS // 2):
        blocks = []
        for chunk in (2 * pair, 2 * pair + 1):
            piece = values[chunk * CHUNK : (chunk + 1) * CHUNK, :]
            tall = jnp.concatenate([piece] * H, axis=0)
            blocks.append(jnp.where(same_head, tall, 0.0).astype(jnp.bfloat16))
        block = jnp.concatenate(blocks, axis=0)
        total = total + jnp.dot(
            mix_ref[:, 2 * pair * LANES : (2 * pair + 2) * LANES], block, preferred_element_type=jnp.float32
        )
    out_ref[...] = total.astype(jnp.bfloat16)


def sample(place, hit_list, mine, other, value_weight, mix):
    return pl.pallas_call(
        sample_kernel,
        out_shape=jax.ShapeDtypeStruct((Q, D), jnp.bfloat16),
        in_specs=[scalars, scalars, whole, whole, whole, whole],
        out_specs=whole,
        compiler_params=pltpu.CompilerParams(vmem_limit_bytes=24 << 20),
        cost_estimate=pl.CostEstimate(flops=1 << 29, bytes_accessed=4 << 20, transcendentals=0),
        name="sample",
    )(place, hit_list, mine, other, value_weight, mix)


def project_kernel(pieces_ref, weight_ref, out_ref):
    total = pieces_ref[0].astype(jnp.float32)
    for i in range(1, CAM_DEVICES):
        total = total + pieces_ref[i].astype(jnp.float32)
    out_ref[...] = jnp.dot(
        total.astype(jnp.bfloat16), weight_ref[...], preferred_element_type=jnp.float32
    ).astype(jnp.bfloat16)


def project(pieces, output_weight):
    return pl.pallas_call(
        project_kernel,
        out_shape=jax.ShapeDtypeStruct((Q // CAM_DEVICES, D), jnp.bfloat16),
        in_specs=[whole, whole],
        out_specs=whole,
        name="project",
    )(pieces, output_weight)


def body(features, value_weight, output_weight, hit_list, sample_index, attention, validity):
    place = jnp.stack([lax.axis_index("core"), lax.axis_index("cam")]).astype(jnp.int32)
    copies = jnp.broadcast_to(features[None], (16, BLOCK, D))
    mine = lax.all_to_all(copies, ("z", "y"), 0, 0, tiled=True).reshape(16 * BLOCK, D)
    index = sample_index.transpose(1, 2, 0)
    mix = build_mix(place, hit_list, index, attention.T, validity.T)
    mine, mix = lax.optimization_barrier((mine, mix))
    other = lax.ppermute(mine, "core", [(0, 1), (1, 0)])
    partial_sums = sample(place, hit_list, mine, other, value_weight, mix)
    pieces = partial_sums.reshape(CAM_DEVICES, Q // CAM_DEVICES, D)
    arrived = lax.all_to_all(pieces, "cam", 0, 0, tiled=True)
    return project(arrived, output_weight)


def solution(mesh):
    split = Mesh(mesh.devices.reshape(8, 2, 2, CAM_DEVICES), ("z", "y", "core", "cam"))
    tile = ("z", "y", "core")
    every = tile + ("cam",)
    in_specs = (
        P(every, None),
        P(),
        P(),
        P(tile, None),
        P(tile, None, None),
        P(tile, None),
        P(tile, None),
    )
    return jax.shard_map(body, mesh=split, in_specs=in_specs, out_specs=P(every, None), check_vma=False)
```

time: 77.2 us -> 42 us (0.54)
  the two profiles are of different devices: /device:TPU:16 before, /device:TPU:1 now
where the time goes in v1:
time: 42 us; the launch traced here: 41.6 us
  starting transfers between devices  14.3 us (34%)
  blocking collectives  10.7 us (25%)
  Pallas kernels  8.5 us (20%)
  local copies, waits for them, and re-layouts  4.56 us (11%)
  waiting for transfers between devices  3.4 us (8%)
    all_to_all x1, starting transfers between devices, body(): lax.all_to_all(copies, ('z', 'y'), 0, 0, tiled=True).reshape(16 * BLOCK, D)  11.7 us
    all_to_all x1, blocking collectives, body(): arrived = lax.all_to_all(pieces, 'cam', 0, 0, tiled=True)  10.7 us
    pallas_call x1, Pallas kernels, build_mix(): pl.pallas_call(mix_kernel, out_shape=jax.ShapeDtypeStruct((Q, CHUNKS * LA...  5.21 us
    unnamed x12, local copies, waits for them, and re-layouts  3.14 us
    ppermute x1, starting transfers between devices, body(): other = lax.ppermute(mine, 'core', [(0, 1), (1, 0)])  2.57 us
    all_to_all x1, waiting for transfers between devices, body(): lax.all_to_all(copies, ('z', 'y'), 0, 0, tiled=True).reshape(16 * BLOCK, D)  2.33 us
    pallas_call x1, Pallas kernels, project(): pl.pallas_call(project_kernel, out_shape=jax.ShapeDtypeStruct((Q // CAM_D...  1.76 us
    pallas_call x1, Pallas kernels, sample(): pl.pallas_call(sample_kernel, out_shape=jax.ShapeDtypeStruct((Q, D), jnp....  1.53 us
  transfers between devices with their start and end apart: 2, of which 2 were waited for; matrix products, arithmetic and copies ran while one was open for 0% of the time, Pallas kernels for 13%

profile of v1, /device:TPU:1, one launch (start us, length us, event | category | flops | bytes accessed | tf_op | source)
XLA Modules:
  0.0 41.6 jit_solution(9370061908286624323)
XLA Ops:
  0.0 0.0 copy-start.5
  0.0 0.0 copy-start.1
  0.0 1.4 %broadcast_in_dim.2 = bf16[16,24,256]{2,1,0:T(8,128)(2,1)} broadcast(bf16[24,256]{1,0:T(8,128)(2,1)} %param.7), dimensions={1,2} | broadcast | bytes 208896 | tf_op jit(solution)/shard_map/broadcast_in_dim | solution.py:162
  1.4 11.7 %all-to-all-start = ((bf16[16,24,256]{2,1,0:T(8,128)(2,1)}), bf16[16,24,256]{2,1,0:T(8,128)(2,1)S(1)}, u32[]{:S(2)}, u32[]{:S(2)}) async-start(bf16[16,24,256]{2,1,0:T(8,128)(2,1)} %broadcast_in_dim.2), calls=%async_computation | async-start | bytes 393216 | tf_op jit(solution)/shard_map/all_to_all | solution.py:163
  13.2 0.1 pad_add_fusion.place_ref
  13.3 0.0 copy-start
  13.3 0.9 %copy-done = s32[512,2,64]{0,2,1:T(8,128)S(1)} copy-done((s32[512,2,64]{0,2,1:T(8,128)S(1)}, s32[512,2,64]{0,2,1:T(8,128)}, u32[]{:S(2)}) %copy-start) | copy-done | bytes 262168
  14.2 0.0 copy-start.2
  14.2 0.8 %copy-done.2 = bf16[512,64]{0,1:T(8,128)(2,1)S(1)} copy-done((bf16[512,64]{0,1:T(8,128)(2,1)S(1)}, bf16[512,64]{0,1:T(8,128)(2,1)}, u32[]{:S(2)}) %copy-start.2) | copy-done | bytes 65560
  15.1 0.0 copy-start.3
  15.1 0.7 %copy-done.3 = s32[512,2]{0,1:T(2,128)S(1)} copy-done((s32[512,2]{0,1:T(2,128)S(1)}, s32[512,2]{0,1:T(2,128)}, u32[]{:S(2)}) %copy-start.3) | copy-done | bytes 4120
  15.7 0.0 copy-start.4
  15.7 0.7 %copy-done.4 = s32[1,2]{1,0:T(1,128)S(1)} copy-done((s32[1,2]{1,0:T(1,128)S(1)}, s32[1,2]{1,0:T(1,128)}, u32[]{:S(2)}) %copy-start.4) | copy-done | bytes 32
  16.4 5.2 %build_mix.1.mix_ref = bf16[512,2304]{1,0:T(8,128)(2,1)S(1)} custom-call(s32[2]{0:T(128)S(1)} %pad_add_fusion.place_ref, s32[1,2]{1,0:T(1,128)S(1)} %copy-done.4, s32[2,64,512]{2,1,0:T(8,128)S(1)} %bitcast.10, bf16[64,512]{1,0:T(8,128)(2,1)S(1)} %bitcast.11, s32[2,512]{1,0:T(2,128)S(1)} %bitcast.12), custom_call_target="tpu_custom_call" | custom-call | flops 536870912 | bytes 4194304 | tf_op jit(solution)/shard_map/build_mix/pallas_call | solution.py:87
  21.6 2.3 %all-to-all-done = bf16[16,24,256]{2,1,0:T(8,128)(2,1)S(1)} async-done(((bf16[16,24,256]{2,1,0:T(8,128)(2,1)}), bf16[16,24,256]{2,1,0:T(8,128)(2,1)S(1)}, u32[]{:S(2)}, u32[]{:S(2)}) %all-to-all-start) | async-done | bytes 196640 | tf_op jit(solution)/shard_map/all_to_all | solution.py:163
  24.0 2.6 %collective-permute-start = (bf16[384,256]{1,0:T(8,128)(2,1)S(1)}, bf16[384,256]{1,0:T(8,128)(2,1)S(1)}, u32[]{:S(2)}, u32[]{:S(2)}) collective-permute-start(bf16[384,256]{1,0:T(8,128)(2,1)S(1)} %bitcast.8), channel_id=1, source_target_pairs={{0,8},{8,0},{1,9},{9,1},{2,10},{10,2},{3,11},{11,3},{4,12},{12,4},... | collective-permute-start | bytes 589832 | tf_op jit(solution)/shard_map/ppermute | solution.py:167
  26.5 1.1 %collective-permute-done.other_ref = bf16[384,256]{1,0:T(8,128)(2,1)S(1)} collective-permute-done((bf16[384,256]{1,0:T(8,128)(2,1)S(1)}, bf16[384,256]{1,0:T(8,128)(2,1)S(1)}, u32[]{:S(2)}, u32[]{:S(2)}) %collective-permute-start) | collective-permute-done | bytes 196640 | tf_op jit(solution)/shard_map/ppermute | solution.py:167
  27.6 0.0 copy-done.5
  27.6 0.0 copy-done.1
  27.6 1.5 %sample.1 = bf16[512,256]{1,0:T(8,128)(2,1)S(1)} custom-call(s32[2]{0:T(128)S(1)} %pad_add_fusion.place_ref, s32[1,2]{1,0:T(1,128)S(1)} %copy-done.5, bf16[384,256]{1,0:T(8,128)(2,1)S(1)} %bitcast.9, bf16[384,256]{1,0:T(8,128)(2,1)S(1)} %collective-permute-done.other_ref, bf16[256,256]{1,0:T(8,128)(2,1)S(1)} %copy-done.1, bf16[512,2304]{1,0:T(8,128)(2,1)S(1)} %build_mix.1.mix_ref), custom_call_target="tpu_custom_call" | custom-call | flops 536870912 | bytes 4194304 | tf_op jit(solution)/shard_map/sample/pallas_call | solution.py:130
  29.1 10.7 %all_to_all.10.pieces_ref = bf16[8,64,256]{2,1,0:T(8,128)(2,1)} all-to-all(bf16[8,64,256]{2,1,0:T(8,128)(2,1)S(1)} %bitcast.7), channel_id=1, replica_groups=mesh['z'=8,'y'=2,'core'=2,'cam'=8] {'cam'}, dimensions={0} | all-to-all | bytes 524288 | tf_op jit(solution)/shard_map/all_to_all | solution.py:170
  39.9 1.8 %project.1 = bf16[64,256]{1,0:T(8,128)(2,1)} custom-call(bf16[8,64,256]{2,1,0:T(8,128)(2,1)} %all_to_all.10.pieces_ref, bf16[256,256]{1,0:T(8,128)(2,1)} %weight_ref.3), custom_call_target="tpu_custom_call" | custom-call | tf_op jit(solution)/shard_map/project/pallas_call | solution.py:151
Async XLA Ops:
  0.0 27.6 %copy-start.5 = (s32[1,2]{1,0:T(1,128)S(1)}, s32[1,2]{1,0:T(1,128)}, u32[]{:S(2)}) copy-start(s32[1,2]{1,0:T(1,128)} %hit_ref.3) | copy-start | bytes 28
  0.0 27.6 %copy-start.1 = (bf16[256,256]{1,0:T(8,128)(2,1)S(1)}, bf16[256,256]{1,0:T(8,128)(2,1)}, u32[]{:S(2)}) copy-start(bf16[256,256]{1,0:T(8,128)(2,1)} %weight_ref.2) | copy-start | bytes 393220
  1.4 22.5 %all-to-all-start = ((bf16[16,24,256]{2,1,0:T(8,128)(2,1)}), bf16[16,24,256]{2,1,0:T(8,128)(2,1)S(1)}, u32[]{:S(2)}, u32[]{:S(2)}) async-start(bf16[16,24,256]{2,1,0:T(8,128)(2,1)} %broadcast_in_dim.2), calls=%async_computation | async-start | bytes 393216 | tf_op jit(solution)/shard_map/all_to_all | solution.py:163
  13.3 1.0 %copy-start = (s32[512,2,64]{0,2,1:T(8,128)S(1)}, s32[512,2,64]{0,2,1:T(8,128)}, u32[]{:S(2)}) copy-start(s32[512,2,64]{0,2,1:T(8,128)} %param.11) | copy-start | bytes 786436
  14.2 0.8 %copy-start.2 = (bf16[512,64]{0,1:T(8,128)(2,1)S(1)}, bf16[512,64]{0,1:T(8,128)(2,1)}, u32[]{:S(2)}) copy-start(bf16[512,64]{0,1:T(8,128)(2,1)} %param.12) | copy-start | bytes 196612
  15.1 0.7 %copy-start.3 = (s32[512,2]{0,1:T(2,128)S(1)}, s32[512,2]{0,1:T(2,128)}, u32[]{:S(2)}) copy-start(s32[512,2]{0,1:T(2,128)} %param.13) | copy-start | bytes 12292
  15.7 0.7 %copy-start.4 = (s32[1,2]{1,0:T(1,128)S(1)}, s32[1,2]{1,0:T(1,128)}, u32[]{:S(2)}) copy-start(s32[1,2]{1,0:T(1,128)} %hit_ref.3) | copy-start | bytes 28
  24.0 3.6 %collective-permute-start = (bf16[384,256]{1,0:T(8,128)(2,1)S(1)}, bf16[384,256]{1,0:T(8,128)(2,1)S(1)}, u32[]{:S(2)}, u32[]{:S(2)}) collective-permute-start(bf16[384,256]{1,0:T(8,128)(2,1)S(1)} %bitcast.8), channel_id=1, source_target_pairs={{0,8},{8,0},{1,9},{9,1},{2,10},{10,2},{3,11},{11,3},{4,12},{12,4},... | collective-permute-start | bytes 589832 | tf_op jit(solution)/shard_map/ppermute | solution.py:167

commit v2 on v1

v2 whole, which is shorter than its diff:
```python
import jax
import jax.numpy as jnp
from jax import lax
from jax.experimental import pallas as pl
from jax.experimental.pallas import tpu as pltpu
from jax.sharding import Mesh, PartitionSpec as P

D = 256
H = 8
K = 8
HITS = 2
CAM_ROWS = 1024
Q = 512
CAM_DEVICES = 8
Z_DEVICES = 8

BLOCK = 24
STRIPE = CAM_DEVICES * BLOCK
QUAD = 2 * BLOCK
HALF = 2 * QUAD
CHUNK = 16
LANES = H * CHUNK
SLOT_CHUNKS = HALF // CHUNK
HALF_CHUNKS = HITS * SLOT_CHUNKS
Q_STEP = 32

whole = pl.BlockSpec(memory_space=pltpu.VMEM)
scalars = pl.BlockSpec(memory_space=pltpu.SMEM)
anywhere = pl.BlockSpec(memory_space=pltpu.HBM)


def first_stripe(camera):
    return (camera * 16) // 3


def mix_kernel(
    place_ref, hit_ref, index_any, attention_any, validity_any, mix_ref,
    index_ref, attention_ref, validity_ref, row_ref, weight_ref, sems,
):
    copies = [
        pltpu.make_async_copy(source, target, sems.at[i])
        for i, (source, target) in enumerate(
            ((index_any, index_ref), (attention_any, attention_ref), (validity_any, validity_ref))
        )
    ]
    for copy in copies:
        copy.start()
    for copy in copies:
        copy.wait()
    y, core, cam = place_ref[0], place_ref[1], place_ref[2]
    hit_count = validity_ref[0:1, :] + validity_ref[1:2, :]
    inverse = 1.0 / jnp.maximum(hit_count, 1).astype(jnp.float32)
    attention = attention_ref[...].astype(jnp.float32)
    rows, weights = [], []
    for slot in range(HITS):
        camera = hit_ref[0, slot]
        stripe = first_stripe(camera)
        shifted = index_ref[slot] + (camera * CAM_ROWS - stripe * STRIPE)
        step = (shifted * 683) >> 17
        within = shifted - step * STRIPE
        owner = (within * 171) >> 12
        tile = step + stripe
        row = within - owner * BLOCK + ((tile >> 2) & 1) * BLOCK
        row = jnp.where((tile & 1) != core, row + QUAD, row)
        row = jnp.where(((tile >> 1) & 1) != y, row + HALF, row)
        row = jnp.where(owner == cam, row, -1)
        rows.append(row.astype(jnp.float32))
        weights.append(attention * validity_ref[slot : slot + 1, :].astype(jnp.float32) * inverse)
    rows = jnp.concatenate(rows, axis=0).T.astype(jnp.bfloat16)
    weights = jnp.concatenate(weights, axis=0).T.astype(jnp.bfloat16)
    source = lax.broadcasted_iota(jnp.int32, (HITS * H * K, LANES), 0)
    lane = lax.broadcasted_iota(jnp.int32, (HITS * H * K, LANES), 1)
    for slot in range(HITS):
        for k in range(K):
            spread = (source == slot * H * K + (lane // CHUNK) * K + k).astype(jnp.bfloat16)
            row_ref[slot * K + k] = jnp.dot(rows, spread, preferred_element_type=jnp.float32).astype(jnp.bfloat16)
            weight_ref[slot * K + k] = jnp.dot(weights, spread, preferred_element_type=jnp.float32).astype(jnp.bfloat16)

    local = lax.broadcasted_iota(jnp.int32, (Q_STEP, LANES), 1) % CHUNK

    @pl.loop(0, Q // Q_STEP)
    def _(step):
        part = pl.ds(pl.multiple_of(step * Q_STEP, Q_STEP), Q_STEP)
        for slot in range(HITS):
            picked = [row_ref[slot * K + k, part, :] for k in range(K)]
            scale = [weight_ref[slot * K + k, part, :] for k in range(K)]
            for half in range(2):
                for i in range(SLOT_CHUNKS):
                    target = (local + (half * HALF + i * CHUNK)).astype(jnp.float32).astype(jnp.bfloat16)
                    total = jnp.zeros((Q_STEP, LANES), jnp.bfloat16)
                    for k in range(K):
                        total = jnp.where(picked[k] == target, scale[k], total)
                    chunk = slot * SLOT_CHUNKS + i
                    mix_ref[half, part, chunk * LANES : (chunk + 1) * LANES] = total


def build_mix(place, hit_list, index, attention, validity):
    return pl.pallas_call(
        mix_kernel,
        out_shape=jax.ShapeDtypeStruct((2, Q, HALF_CHUNKS * LANES), jnp.bfloat16),
        in_specs=[scalars, scalars, anywhere, anywhere, anywhere],
        out_specs=whole,
        scratch_shapes=[
            pltpu.VMEM((HITS, H * K, Q), jnp.int32),
            pltpu.VMEM((H * K, Q), jnp.bfloat16),
            pltpu.VMEM((HITS, Q), jnp.int32),
            pltpu.VMEM((HITS * K, Q, LANES), jnp.bfloat16),
            pltpu.VMEM((HITS * K, Q, LANES), jnp.bfloat16),
            pltpu.SemaphoreType.DMA((3,)),
        ],
        compiler_params=pltpu.CompilerParams(vmem_limit_bytes=16 << 20),
        cost_estimate=pl.CostEstimate(flops=1 << 29, bytes_accessed=4 << 20, transcendentals=0),
        name="build_mix",
    )(place, hit_list, index, attention, validity)


def mixed(place_ref, hit_ref, mine_ref, other_ref, weight_ref, mix, y):
    core = place_ref[1]
    blocks = []
    for slot in range(HITS):
        stripe = first_stripe(hit_ref[0, slot])
        for ref, place_core in ((mine_ref, core), (other_ref, 1 - core)):
            place = 2 * y + place_core
            first = (stripe + ((place - stripe) & 3) - place) // 4
            first = jnp.minimum(first, Z_DEVICES - 2)
            for parity in range(2):
                z = first + ((first + parity) & 1)
                blocks.append(ref[pl.ds(pl.multiple_of(z * BLOCK, 8), BLOCK), :])
    features = jnp.concatenate(blocks, axis=0)
    values = jnp.dot(features, weight_ref[...], preferred_element_type=jnp.float32)
    head_of_row = lax.broadcasted_iota(jnp.int32, (LANES, D), 0) // CHUNK
    head_of_column = lax.broadcasted_iota(jnp.int32, (LANES, D), 1) // (D // H)
    same_head = head_of_row == head_of_column
    total = jnp.zeros((Q, D), jnp.float32)
    for pair in range(HALF_CHUNKS // 2):
        blocks = []
        for chunk in (2 * pair, 2 * pair + 1):
            piece = values[chunk * CHUNK : (chunk + 1) * CHUNK, :]
            tall = jnp.concatenate([piece] * H, axis=0)
            blocks.append(jnp.where(same_head, tall, 0.0).astype(jnp.bfloat16))
        block = jnp.concatenate(blocks, axis=0)
        columns = slice(2 * pair * LANES, (2 * pair + 2) * LANES)
        total = total + jnp.dot(mix[:, columns], block, preferred_element_type=jnp.float32)
    return total


def near_kernel(place_ref, hit_ref, mine_ref, other_ref, weight_ref, mix_ref, out_ref):
    out_ref[...] = mixed(place_ref, hit_ref, mine_ref, other_ref, weight_ref, mix_ref.at[0], place_ref[0])


def far_kernel(place_ref, hit_ref, mine_ref, other_ref, weight_ref, mix_ref, near_ref, out_ref):
    total = mixed(place_ref, hit_ref, mine_ref, other_ref, weight_ref, mix_ref.at[1], 1 - place_ref[0])
    out_ref[...] = (near_ref[...] + total).astype(jnp.bfloat16)


def sample(kernel, kind, name, *operands):
    return pl.pallas_call(
        kernel,
        out_shape=jax.ShapeDtypeStruct((Q, D), kind),
        in_specs=[scalars, scalars] + [whole] * (len(operands) - 2),
        out_specs=whole,
        compiler_params=pltpu.CompilerParams(vmem_limit_bytes=16 << 20),
        cost_estimate=pl.CostEstimate(flops=1 << 29, bytes_accessed=2 << 20, transcendentals=0),
        name=name,
    )(*operands)


def project_kernel(pieces_ref, weight_ref, out_ref):
    total = pieces_ref[0].astype(jnp.float32)
    for i in range(1, CAM_DEVICES):
        total = total + pieces_ref[i].astype(jnp.float32)
    out_ref[...] = jnp.dot(
        total.astype(jnp.bfloat16), weight_ref[...], preferred_element_type=jnp.float32
    ).astype(jnp.bfloat16)


def project(pieces, output_weight):
    return pl.pallas_call(
        project_kernel,
        out_shape=jax.ShapeDtypeStruct((Q // CAM_DEVICES, D), jnp.bfloat16),
        in_specs=[whole, whole],
        out_specs=whole,
        compiler_params=pltpu.CompilerParams(vmem_limit_bytes=8 << 20),
        name="project",
    )(pieces, output_weight)


def swapped(x, axis):
    return lax.ppermute(x, axis, [(0, 1), (1, 0)])


def body(features, value_weight, output_weight, hit_list, sample_index, attention, validity):
    place = jnp.stack([lax.axis_index("y"), lax.axis_index("core"), lax.axis_index("cam")]).astype(jnp.int32)
    copies = jnp.broadcast_to(features[None], (Z_DEVICES, BLOCK, D))
    mine = lax.all_to_all(copies, "z", 0, 0, tiled=True).reshape(Z_DEVICES * BLOCK, D)
    mix = build_mix(place, hit_list, sample_index.transpose(1, 2, 0), attention.T, validity.T)
    mine, mix = lax.optimization_barrier((mine, mix))
    far_mine = swapped(mine, "y")
    other = swapped(mine, "core")
    near = sample(near_kernel, jnp.float32, "sample_near", place, hit_list, mine, other, value_weight, mix)
    far_mine, near = lax.optimization_barrier((far_mine, near))
    far_other = swapped(far_mine, "core")
    partial_sums = sample(
        far_kernel, jnp.bfloat16, "sample_far", place, hit_list, far_mine, far_other, value_weight, mix, near
    )
    pieces = partial_sums.reshape(CAM_DEVICES, Q // CAM_DEVICES, D)
    arrived = lax.all_to_all(pieces, "cam", 0, 0, tiled=True)
    return project(arrived, output_weight)


def solution(mesh):
    split = Mesh(mesh.devices.reshape(Z_DEVICES, 2, 2, CAM_DEVICES), ("z", "y", "core", "cam"))
    tile = ("z", "y", "core")
    every = tile + ("cam",)
    in_specs = (
        P(every, None),
        P(),
        P(),
        P(tile, None),
        P(tile, None, None),
        P(tile, None),
        P(tile, None),
    )
    return jax.shard_map(body, mesh=split, in_specs=in_specs, out_specs=P(every, None), check_vma=False)
```

time: 42 us -> 42.4 us (level)
  blocking collectives: 10.7 us -> 11.9 us
  waiting for transfers between devices: 3.4 us -> 2.54 us
  Pallas kernels: 8.5 us -> 9.19 us
    all_to_all x1, starting transfers between devices: 11.7 us -> 9.01 us  [body(): lax.all_to_all(copies, 'z', 0, 0, tiled=True).reshape(Z_DEVICES * BLOCK, D)]
    all_to_all x1, waiting for transfers between devices: 2.33 us -> 0.01 us  [body(): lax.all_to_all(copies, 'z', 0, 0, tiled=True).reshape(Z_DEVICES * BLOCK, D)]
    ppermute x1 -> x3, starting transfers between devices: 2.57 us -> 4.85 us  [swapped(): return lax.ppermute(x, axis, [(0, 1), (1, 0)])]
    pallas_call x2 -> x3, Pallas kernels: 6.74 us -> 8.41 us  [the longest x1 5.79 us: build_mix(): pl.pallas_call(mix_kernel, out_shape=jax.ShapeDtypeStruct((2, Q, HALF_CHU...]
    ppermute x1 -> x3, waiting for transfers between devices: 1.07 us -> 2.54 us  [swapped(): return lax.ppermute(x, axis, [(0, 1), (1, 0)])]
    all_to_all x1, blocking collectives: 10.7 us -> 11.9 us  [body(): arrived = lax.all_to_all(pieces, 'cam', 0, 0, tiled=True)]
    pallas_call x1, Pallas kernels: 1.76 us -> 0.78 us  [project(): pl.pallas_call(project_kernel, out_shape=jax.ShapeDtypeStruct((Q // CAM_D...]
    unnamed x12 -> x14, local copies, waits for them, and re-layouts: 3.14 us -> 3.14 us
  transfers between devices with their start and end apart: 2 -> 4, of which waited for: 2 -> 2; matrix products, arithmetic and copies ran while one was open for 0% -> 0% of each run, Pallas kernels for 13% -> 17%
where the time goes in v2:
time: 42.4 us; the launch traced here: 42.1 us
  starting transfers between devices  13.9 us (33%)
  blocking collectives  11.9 us (28%)
  Pallas kernels  9.19 us (22%)
  local copies, waits for them, and re-layouts  4.53 us (11%)
  waiting for transfers between devices  2.54 us (6%)
    all_to_all x1, blocking collectives, body(): arrived = lax.all_to_all(pieces, 'cam', 0, 0, tiled=True)  11.9 us
    all_to_all x1, starting transfers between devices, body(): lax.all_to_all(copies, 'z', 0, 0, tiled=True).reshape(Z_DEVICES * BLOCK, D)  9.01 us
    pallas_call x1, Pallas kernels, build_mix(): pl.pallas_call(mix_kernel, out_shape=jax.ShapeDtypeStruct((2, Q, HALF_CHU...  5.79 us
    ppermute x3, starting transfers between devices, swapped(): return lax.ppermute(x, axis, [(0, 1), (1, 0)])  4.85 us
    unnamed x14, local copies, waits for them, and re-layouts  3.14 us
    pallas_call x2, Pallas kernels, sample(): pl.pallas_call(kernel, out_shape=jax.ShapeDtypeStruct((Q, D), kind), in_s...  2.62 us
    ppermute x3, waiting for transfers between devices, swapped(): return lax.ppermute(x, axis, [(0, 1), (1, 0)])  2.54 us
    broadcast_in_dim x1, local copies, waits for them, and re-layouts, body(): copies = jnp.broadcast_to(features[None], (Z_DEVICES, BLOCK, D))  1.38 us
  transfers between devices with their start and end apart: 4, of which 2 were waited for; matrix products, arithmetic and copies ran while one was open for 0% of the time, Pallas kernels for 17%

profile of v2, /device:TPU:1, one launch (start us, length us, event | category | flops | bytes accessed | tf_op | source)
XLA Modules:
  0.0 42.1 jit_solution(13033825079480986345)
XLA Ops:
  0.0 0.0 copy-start.5
  0.0 1.4 %broadcast_in_dim.2 = bf16[8,24,256]{2,1,0:T(8,128)(2,1)} broadcast(bf16[24,256]{1,0:T(8,128)(2,1)} %param.7), dimensions={1,2} | broadcast | bytes 110592 | tf_op jit(solution)/shard_map/broadcast_in_dim | solution.py:194
  1.4 9.0 %all-to-all-start = ((bf16[8,24,256]{2,1,0:T(8,128)(2,1)}), bf16[8,24,256]{2,1,0:T(8,128)(2,1)S(1)}, u32[]{:S(2)}, u32[]{:S(2)}) async-start(bf16[8,24,256]{2,1,0:T(8,128)(2,1)} %broadcast_in_dim.2), calls=%async_computation | async-start | bytes 196608 | tf_op jit(solution)/shard_map/all_to_all | solution.py:195
  10.4 0.1 pad_add_fusion.place_ref
  10.5 0.9 %copy-done.1 = s32[512,2,64]{0,2,1:T(8,128)S(1)} copy-done((s32[512,2,64]{0,2,1:T(8,128)S(1)}, s32[512,2,64]{0,2,1:T(8,128)}, u32[]{:S(2)}) %copy-start.1) | copy-done | bytes 262168
  11.4 0.8 %copy-done.3 = bf16[512,64]{0,1:T(8,128)(2,1)S(1)} copy-done((bf16[512,64]{0,1:T(8,128)(2,1)S(1)}, bf16[512,64]{0,1:T(8,128)(2,1)}, u32[]{:S(2)}) %copy-start.3) | copy-done | bytes 65560
  12.3 0.7 %copy-done.4 = s32[1,2]{1,0:T(1,128)S(1)} copy-done((s32[1,2]{1,0:T(1,128)S(1)}, s32[1,2]{1,0:T(1,128)}, u32[]{:S(2)}) %copy-start.4) | copy-done | bytes 32
  12.9 0.7 %copy-done.6 = s32[512,2]{0,1:T(2,128)S(1)} copy-done((s32[512,2]{0,1:T(2,128)S(1)}, s32[512,2]{0,1:T(2,128)}, u32[]{:S(2)}) %copy-start.6) | copy-done | bytes 4120
  13.6 5.8 %build_mix.1.mix_ref = bf16[2,512,1536]{2,1,0:T(8,128)(2,1)S(1)} custom-call(s32[3]{0:T(128)S(1)} %pad_add_fusion.place_ref, s32[1,2]{1,0:T(1,128)S(1)} %copy-done.4, s32[2,64,512]{2,1,0:T(8,128)S(1)} %bitcast.12, bf16[64,512]{1,0:T(8,128)(2,1)S(1)} %bitcast.13, s32[2,512]{1,0:T(2,128)S(1)} %bitcast.14), custom_call_target="tpu_custom_call" | custom-call | flops 536870912 | bytes 4194304 | tf_op jit(solution)/shard_map/build_mix/pallas_call | solution.py:98
  19.4 0.0 all-to-all-done
  19.4 1.0 %collective-permute-start.1 = (bf16[192,256]{1,0:T(8,128)(2,1)S(1)}, bf16[192,256]{1,0:T(8,128)(2,1)S(1)}, u32[]{:S(2)}, u32[]{:S(2)}) collective-permute-start(bf16[192,256]{1,0:T(8,128)(2,1)S(1)} %bitcast.9), channel_id=1, source_target_pairs={{0,8},{8,0},{1,9},{9,1},{2,10},{10,2},{3,11},{11,3},{4,12},{12,4},... | collective-permute-start | bytes 294920 | tf_op jit(solution)/shard_map/ppermute | solution.py:189
  20.5 2.9 %collective-permute-start = (bf16[192,256]{1,0:T(8,128)(2,1)S(1)}, bf16[192,256]{1,0:T(8,128)(2,1)S(1)}, u32[]{:S(2)}, u32[]{:S(2)}) collective-permute-start(bf16[192,256]{1,0:T(8,128)(2,1)S(1)} %bitcast.10), channel_id=1, source_target_pairs={{0,16},{16,0},{1,17},{17,1},{2,18},{18,2},{3,19},{19,3},{4,20},{20... | collective-permute-start | bytes 294920 | tf_op jit(solution)/shard_map/ppermute | solution.py:189
  23.4 0.0 collective-permute-done.1.other_ref
  23.4 0.0 copy-done.5
  23.4 0.0 copy-done
  23.4 1.3 %sample_near.1.near_ref = f32[512,256]{1,0:T(8,128)S(1)} custom-call(s32[3]{0:T(128)S(1)} %pad_add_fusion.place_ref, s32[1,2]{1,0:T(1,128)S(1)} %copy-done.5, bf16[192,256]{1,0:T(8,128)(2,1)S(1)} %bitcast.11, bf16[192,256]{1,0:T(8,128)(2,1)S(1)} %collective-permute-done.1.other_ref, bf16[256,256]{1,0:T(8,128)(2,1)S(1)} %copy-done, ...), custom_call_target="tpu_custom_call" | custom-call | flops 536870912 | bytes 2097152 | tf_op jit(solution)/shard_map/sample_near/pallas_call | solution.py:157
  24.7 0.0 copy-start.2
  24.7 1.6 %collective-permute-done.mine_ref = bf16[192,256]{1,0:T(8,128)(2,1)S(1)} collective-permute-done((bf16[192,256]{1,0:T(8,128)(2,1)S(1)}, bf16[192,256]{1,0:T(8,128)(2,1)S(1)}, u32[]{:S(2)}, u32[]{:S(2)}) %collective-permute-start) | collective-permute-done | bytes 98336 | tf_op jit(solution)/shard_map/ppermute | solution.py:189
  26.3 0.9 %collective-permute-start.2 = (bf16[192,256]{1,0:T(8,128)(2,1)S(1)}, bf16[192,256]{1,0:T(8,128)(2,1)S(1)}, u32[]{:S(2)}, u32[]{:S(2)}) collective-permute-start(bf16[192,256]{1,0:T(8,128)(2,1)S(1)} %collective-permute-done.mine_ref), channel_id=1, source_target_pairs={{0,8},{8,0},{1,9},{9,1},{2,10},{10,2},{3,11},{11,3},{4,12},{12,4},... | collective-permute-start | bytes 294920 | tf_op jit(solution)/shard_map/ppermute | solution.py:189
  27.2 0.9 %collective-permute-done.2.other_ref = bf16[192,256]{1,0:T(8,128)(2,1)S(1)} collective-permute-done((bf16[192,256]{1,0:T(8,128)(2,1)S(1)}, bf16[192,256]{1,0:T(8,128)(2,1)S(1)}, u32[]{:S(2)}, u32[]{:S(2)}) %collective-permute-start.2) | collective-permute-done | bytes 98336 | tf_op jit(solution)/shard_map/ppermute | solution.py:189
  28.1 1.3 %sample_far.1 = bf16[512,256]{1,0:T(8,128)(2,1)S(1)} custom-call(s32[3]{0:T(128)S(1)} %pad_add_fusion.place_ref, s32[1,2]{1,0:T(1,128)S(1)} %copy-done.5, bf16[192,256]{1,0:T(8,128)(2,1)S(1)} %collective-permute-done.mine_ref, bf16[192,256]{1,0:T(8,128)(2,1)S(1)} %collective-permute-done.2.other_ref, bf16[256,256]{1,0:T(8,128)(2,1)S(1)} %copy-done, ...), custom_call_target="tpu_custom_call" | custom-call | flops 536870912 | bytes 2097152 | tf_op jit(solution)/shard_map/sample_far/pallas_call | solution.py:157
  29.5 11.9 %all_to_all.10.pieces_ref = bf16[8,64,256]{2,1,0:T(8,128)(2,1)S(1)} all-to-all(bf16[8,64,256]{2,1,0:T(8,128)(2,1)S(1)} %bitcast.8), channel_id=1, replica_groups=mesh['z'=8,'y'=2,'core'=2,'cam'=8] {'cam'}, dimensions={0} | all-to-all | bytes 524288 | tf_op jit(solution)/shard_map/all_to_all | solution.py:207
  41.3 0.0 copy-done.2
  41.3 0.8 %project.1 = bf16[64,256]{1,0:T(8,128)(2,1)} custom-call(bf16[8,64,256]{2,1,0:T(8,128)(2,1)S(1)} %all_to_all.10.pieces_ref, bf16[256,256]{1,0:T(8,128)(2,1)S(1)} %copy-done.2), custom_call_target="tpu_custom_call" | custom-call | tf_op jit(solution)/shard_map/project/pallas_call | solution.py:178
  (5 shorter events, 0.0 us)
Async XLA Ops:
  0.0 23.4 %copy-start.5 = (s32[1,2]{1,0:T(1,128)S(1)}, s32[1,2]{1,0:T(1,128)}, u32[]{:S(2)}) copy-start(s32[1,2]{1,0:T(1,128)} %hit_ref.5) | copy-start | bytes 28
  0.0 23.4 %copy-start = (bf16[256,256]{1,0:T(8,128)(2,1)S(1)}, bf16[256,256]{1,0:T(8,128)(2,1)}, u32[]{:S(2)}) copy-start(bf16[256,256]{1,0:T(8,128)(2,1)} %weight_ref.4) | copy-start | bytes 393220
  1.4 18.0 %all-to-all-start = ((bf16[8,24,256]{2,1,0:T(8,128)(2,1)}), bf16[8,24,256]{2,1,0:T(8,128)(2,1)S(1)}, u32[]{:S(2)}, u32[]{:S(2)}) async-start(bf16[8,24,256]{2,1,0:T(8,128)(2,1)} %broadcast_in_dim.2), calls=%async_computation | async-start | bytes 196608 | tf_op jit(solution)/shard_map/all_to_all | solution.py:195
  10.5 1.0 %copy-start.1 = (s32[512,2,64]{0,2,1:T(8,128)S(1)}, s32[512,2,64]{0,2,1:T(8,128)}, u32[]{:S(2)}) copy-start(s32[512,2,64]{0,2,1:T(8,128)} %param.11) | copy-start | bytes 786436
  11.4 0.8 %copy-start.3 = (bf16[512,64]{0,1:T(8,128)(2,1)S(1)}, bf16[512,64]{0,1:T(8,128)(2,1)}, u32[]{:S(2)}) copy-start(bf16[512,64]{0,1:T(8,128)(2,1)} %param.12) | copy-start | bytes 196612
  12.3 0.7 %copy-start.4 = (s32[1,2]{1,0:T(1,128)S(1)}, s32[1,2]{1,0:T(1,128)}, u32[]{:S(2)}) copy-start(s32[1,2]{1,0:T(1,128)} %hit_ref.5) | copy-start | bytes 28
  12.9 0.7 %copy-start.6 = (s32[512,2]{0,1:T(2,128)S(1)}, s32[512,2]{0,1:T(2,128)}, u32[]{:S(2)}) copy-start(s32[512,2]{0,1:T(2,128)} %param.13) | copy-start | bytes 12292
  19.4 4.0 %collective-permute-start.1 = (bf16[192,256]{1,0:T(8,128)(2,1)S(1)}, bf16[192,256]{1,0:T(8,128)(2,1)S(1)}, u32[]{:S(2)}, u32[]{:S(2)}) collective-permute-start(bf16[192,256]{1,0:T(8,128)(2,1)S(1)} %bitcast.9), channel_id=1, source_target_pairs={{0,8},{8,0},{1,9},{9,1},{2,10},{10,2},{3,11},{11,3},{4,12},{12,4},... | collective-permute-start | bytes 294920 | tf_op jit(solution)/shard_map/ppermute | solution.py:189
  20.5 5.9 %collective-permute-start = (bf16[192,256]{1,0:T(8,128)(2,1)S(1)}, bf16[192,256]{1,0:T(8,128)(2,1)S(1)}, u32[]{:S(2)}, u32[]{:S(2)}) collective-permute-start(bf16[192,256]{1,0:T(8,128)(2,1)S(1)} %bitcast.10), channel_id=1, source_target_pairs={{0,16},{16,0},{1,17},{17,1},{2,18},{18,2},{3,19},{19,3},{4,20},{20... | collective-permute-start | bytes 294920 | tf_op jit(solution)/shard_map/ppermute | solution.py:189
  24.7 16.6 %copy-start.2 = (bf16[256,256]{1,0:T(8,128)(2,1)S(1)}, bf16[256,256]{1,0:T(8,128)(2,1)}, u32[]{:S(2)}) copy-start(bf16[256,256]{1,0:T(8,128)(2,1)} %weight_ref.5) | copy-start | bytes 393220
  26.3 1.8 %collective-permute-start.2 = (bf16[192,256]{1,0:T(8,128)(2,1)S(1)}, bf16[192,256]{1,0:T(8,128)(2,1)S(1)}, u32[]{:S(2)}, u32[]{:S(2)}) collective-permute-start(bf16[192,256]{1,0:T(8,128)(2,1)S(1)} %collective-permute-done.mine_ref), channel_id=1, source_target_pairs={{0,8},{8,0},{1,9},{9,1},{2,10},{10,2},{3,11},{11,3},{4,12},{12,4},... | collective-permute-start | bytes 294920 | tf_op jit(solution)/shard_map/ppermute | solution.py:189

commit v3 on v2

v3 whole, which is shorter than its diff:
```python
import jax
import jax.numpy as jnp
from jax import lax
from jax.experimental import pallas as pl
from jax.experimental.pallas import tpu as pltpu
from jax.sharding import Mesh, PartitionSpec as P

D = 256
H = 8
K = 8
HITS = 2
CAM_ROWS = 1024
Q = 512
CAM_DEVICES = 8
ZY_DEVICES = 16

BLOCK = 24
STRIPE = CAM_DEVICES * BLOCK
STRIPES = 6
WINDOW = STRIPES * BLOCK
CHUNK = 16
LANES = H * CHUNK
CHUNKS = HITS * WINDOW // CHUNK
Q_STEP = 32

whole = pl.BlockSpec(memory_space=pltpu.VMEM)
scalars = pl.BlockSpec(memory_space=pltpu.SMEM)
anywhere = pl.BlockSpec(memory_space=pltpu.HBM)


def first_stripe(camera):
    return (camera * 16) // 3


def mix_kernel(
    place_ref, hit_any, index_any, attention_any, validity_any, mix_ref,
    hit_ref, index_ref, attention_ref, validity_ref, row_ref, weight_ref, sems,
):
    copies = [
        pltpu.make_async_copy(source, target, sems.at[i])
        for i, (source, target) in enumerate(
            (
                (index_any, index_ref),
                (attention_any, attention_ref),
                (validity_any, validity_ref),
                (hit_any, hit_ref),
            )
        )
    ]
    for copy in copies:
        copy.start()
    for copy in copies:
        copy.wait()
    cam = place_ref[1]
    hit_count = validity_ref[0:1, :] + validity_ref[1:2, :]
    inverse = 1.0 / jnp.maximum(hit_count, 1).astype(jnp.float32)
    attention = attention_ref[...].astype(jnp.float32)
    rows, weights = [], []
    for slot in range(HITS):
        camera = hit_ref[0, slot]
        shifted = index_ref[slot] + (camera * CAM_ROWS - first_stripe(camera) * STRIPE)
        stripe = (shifted * 683) >> 17
        within = shifted - stripe * STRIPE
        owner = (within * 171) >> 12
        row = within - owner * BLOCK + stripe * BLOCK
        row = jnp.where(owner == cam, row, -2 * CHUNK)
        rows.append(row.astype(jnp.float32))
        weights.append(attention * validity_ref[slot : slot + 1, :].astype(jnp.float32) * inverse)
    rows = jnp.concatenate(rows, axis=0).T.astype(jnp.bfloat16)
    weights = jnp.concatenate(weights, axis=0).T.astype(jnp.bfloat16)
    source = lax.broadcasted_iota(jnp.int32, (HITS * H * K, LANES), 0)
    lane = lax.broadcasted_iota(jnp.int32, (HITS * H * K, LANES), 1)
    for slot in range(HITS):
        for k in range(K):
            spread = (source == slot * H * K + (lane // CHUNK) * K + k).astype(jnp.bfloat16)
            spread_rows = jnp.dot(rows, spread, preferred_element_type=jnp.float32)
            row_ref[slot * K + k] = spread_rows.astype(jnp.int32).astype(jnp.int16)
            spread_weights = jnp.dot(weights, spread, preferred_element_type=jnp.float32)
            weight_ref[slot * K + k] = spread_weights.astype(jnp.bfloat16)

    local = lax.broadcasted_iota(jnp.int32, (Q_STEP, LANES), 1) % CHUNK

    @pl.loop(0, Q // Q_STEP)
    def _(step):
        part = pl.ds(pl.multiple_of(step * Q_STEP, Q_STEP), Q_STEP)
        for slot in range(HITS):
            picked = [row_ref[slot * K + k, part, :] for k in range(K)]
            scale = [weight_ref[slot * K + k, part, :] for k in range(K)]
            for chunk in slot_chunks(slot):
                target = (local + (chunk * CHUNK - slot * WINDOW)).astype(jnp.int16)
                total = jnp.zeros((Q_STEP, LANES), jnp.bfloat16)
                for k in range(K):
                    total = jnp.where(picked[k] == target, scale[k], total)
                mix_ref[part, chunk * LANES : (chunk + 1) * LANES] = total


def slot_chunks(slot):
    return range(slot * WINDOW // CHUNK, (slot + 1) * WINDOW // CHUNK)


def build_mix(place, hit_list, index, attention, validity):
    inputs = (pltpu.with_memory_space_constraint(x, pltpu.HBM) for x in (hit_list, index, attention, validity))
    return pl.pallas_call(
        mix_kernel,
        out_shape=jax.ShapeDtypeStruct((Q, CHUNKS * LANES), jnp.bfloat16),
        in_specs=[scalars, anywhere, anywhere, anywhere, anywhere],
        out_specs=whole,
        scratch_shapes=[
            pltpu.SMEM((1, HITS), jnp.int32),
            pltpu.VMEM((HITS, H * K, Q), jnp.int32),
            pltpu.VMEM((H * K, Q), jnp.bfloat16),
            pltpu.VMEM((HITS, Q), jnp.int32),
            pltpu.VMEM((HITS * K, Q, LANES), jnp.int16),
            pltpu.VMEM((HITS * K, Q, LANES), jnp.bfloat16),
            pltpu.SemaphoreType.DMA((4,)),
        ],
        compiler_params=pltpu.CompilerParams(vmem_limit_bytes=16 << 20),
        cost_estimate=pl.CostEstimate(flops=1 << 29, bytes_accessed=4 << 20, transcendentals=0),
        name="build_mix",
    )(place, *inputs)


def sample_kernel(place_ref, hit_ref, mine_ref, other_ref, weight_ref, mix_ref, out_ref):
    core = place_ref[0]
    blocks = []
    for slot in range(HITS):
        first = first_stripe(hit_ref[0, slot])
        for i in range(STRIPES):
            tile = first + i
            part = pl.ds(pl.multiple_of((ZY_DEVICES - 1 - (tile >> 1)) * BLOCK, 8), BLOCK)
            blocks.append(jnp.where((tile & 1) == core, mine_ref[part, :], other_ref[part, :]))
    features = jnp.concatenate(blocks, axis=0)
    values = jnp.dot(features, weight_ref[...], preferred_element_type=jnp.float32)
    head_of_row = lax.broadcasted_iota(jnp.int32, (LANES, D), 0) // CHUNK
    head_of_column = lax.broadcasted_iota(jnp.int32, (LANES, D), 1) // (D // H)
    same_head = head_of_row == head_of_column
    total = jnp.zeros((Q, D), jnp.float32)
    for pair in range(CHUNKS // 2):
        blocks = []
        for chunk in (2 * pair, 2 * pair + 1):
            piece = values[chunk * CHUNK : (chunk + 1) * CHUNK, :]
            tall = jnp.concatenate([piece] * H, axis=0)
            blocks.append(jnp.where(same_head, tall, 0.0).astype(jnp.bfloat16))
        block = jnp.concatenate(blocks, axis=0)
        columns = slice(2 * pair * LANES, (2 * pair + 2) * LANES)
        total = total + jnp.dot(mix_ref[:, columns], block, preferred_element_type=jnp.float32)
    total = total.astype(jnp.bfloat16)
    share = Q // CAM_DEVICES
    for i in range(CAM_DEVICES):
        out_ref[CAM_DEVICES - 1 - i] = total[i * share : (i + 1) * share, :]


def sample(*operands):
    return pl.pallas_call(
        sample_kernel,
        out_shape=jax.ShapeDtypeStruct((CAM_DEVICES, Q // CAM_DEVICES, D), jnp.bfloat16),
        in_specs=[scalars, scalars, whole, whole, whole, whole],
        out_specs=whole,
        compiler_params=pltpu.CompilerParams(vmem_limit_bytes=16 << 20),
        cost_estimate=pl.CostEstimate(flops=1 << 29, bytes_accessed=2 << 20, transcendentals=0),
        name="sample",
    )(*operands)


def project_kernel(pieces_ref, weight_ref, out_ref):
    total = pieces_ref[0].astype(jnp.float32)
    for i in range(1, CAM_DEVICES):
        total = total + pieces_ref[i].astype(jnp.float32)
    out_ref[...] = jnp.dot(
        total.astype(jnp.bfloat16), weight_ref[...], preferred_element_type=jnp.float32
    ).astype(jnp.bfloat16)


def project(pieces, output_weight):
    return pl.pallas_call(
        project_kernel,
        out_shape=jax.ShapeDtypeStruct((Q // CAM_DEVICES, D), jnp.bfloat16),
        in_specs=[whole, whole],
        out_specs=whole,
        compiler_params=pltpu.CompilerParams(vmem_limit_bytes=8 << 20),
        name="project",
    )(pieces, output_weight)


def swapped(x, axis):
    return lax.ppermute(x, axis, [(0, 1), (1, 0)])


def exchanged(x, axis, order):
    return lax.all_to_all(x, axis, 0, 0, tiled=True, axis_index_groups=[order])


def body(features, value_weight, output_weight, hit_list, sample_index, attention, validity):
    place = jnp.stack([lax.axis_index("core"), lax.axis_index("cam")]).astype(jnp.int32)
    copies = jnp.broadcast_to(features[None], (ZY_DEVICES, BLOCK, D))
    mine = exchanged(copies, "zy", list(reversed(range(ZY_DEVICES)))).reshape(ZY_DEVICES * BLOCK, D)
    mix = build_mix(place, hit_list, sample_index.transpose(1, 2, 0), attention.T, validity.T)
    mine, mix = lax.optimization_barrier((mine, mix))
    other = swapped(mine, "core")
    pieces = sample(place, hit_list, mine, other, value_weight, mix)
    arrived = exchanged(pieces, "cam", list(reversed(range(CAM_DEVICES))))
    return project(arrived, output_weight)


def solution(mesh):
    split = Mesh(mesh.devices.reshape(ZY_DEVICES, 2, CAM_DEVICES), ("zy", "core", "cam"))
    tile = ("zy", "core")
    every = tile + ("cam",)
    in_specs = (
        P(every, None),
        P(),
        P(),
        P(tile, None),
        P(tile, None, None),
        P(tile, None),
        P(tile, None),
    )
    return jax.shard_map(body, mesh=split, in_specs=in_specs, out_specs=P(every, None), check_vma=False)
```

time: 42.4 us -> 35.7 us (0.84)
  the two profiles are of different devices: /device:TPU:1 before, /device:TPU:16 now
where the time goes in v3:
time: 35.7 us; the launch traced here: 35.4 us
  blocking collectives  11.2 us (31%)
  starting transfers between devices  9.26 us (26%)
  Pallas kernels  8.01 us (22%)
  waiting for transfers between devices  5.41 us (15%)
  local copies, waits for them, and re-layouts  1.44 us (4%)
    all_to_all x1, blocking collectives, exchanged(): return lax.all_to_all(x, axis, 0, 0, tiled=True, axis_index_groups=[order])  11.2 us
    all_to_all x1, starting transfers between devices, exchanged(): return lax.all_to_all(x, axis, 0, 0, tiled=True, axis_index_groups=[order])  9.25 us
    pallas_call x1, Pallas kernels, build_mix(): pl.pallas_call(mix_kernel, out_shape=jax.ShapeDtypeStruct((Q, CHUNKS * LA...  5.69 us
    all_to_all x1, waiting for transfers between devices, exchanged(): return lax.all_to_all(x, axis, 0, 0, tiled=True, axis_index_groups=[order])  3.97 us
    pallas_call x1, Pallas kernels, sample(): pl.pallas_call(sample_kernel, out_shape=jax.ShapeDtypeStruct((CAM_DEVICES...  1.53 us
    ppermute x1, waiting for transfers between devices, swapped(): return lax.ppermute(x, axis, [(0, 1), (1, 0)])  1.44 us
    broadcast_in_dim x1, local copies, waits for them, and re-layouts, body(): copies = jnp.broadcast_to(features[None], (ZY_DEVICES, BLOCK, D))  1.42 us
    pallas_call x1, Pallas kernels, project(): pl.pallas_call(project_kernel, out_shape=jax.ShapeDtypeStruct((Q // CAM_D...  0.78 us
  transfers between devices with their start and end apart: 2, of which 2 were waited for; matrix products, arithmetic and copies ran while one was open for 0% of the time, Pallas kernels for 16%

profile of v3, /device:TPU:16, one launch (start us, length us, event | category | flops | bytes accessed | tf_op | source)
XLA Modules:
  0.0 35.4 jit_solution(10274754016765182221)
XLA Ops:
  0.0 0.0 copy-start.2
  0.0 0.0 copy-start
  0.0 1.4 %broadcast_in_dim.2 = bf16[16,24,256]{2,1,0:T(8,128)(2,1)} broadcast(bf16[24,256]{1,0:T(8,128)(2,1)} %param.7), dimensions={1,2} | broadcast | bytes 208896 | tf_op jit(solution)/shard_map/broadcast_in_dim | solution.py:195
  1.4 9.3 %all-to-all-start = ((bf16[16,24,256]{2,1,0:T(8,128)(2,1)}), bf16[16,24,256]{2,1,0:T(8,128)(2,1)S(1)}, u32[]{:S(2)}, u32[]{:S(2)}) async-start(bf16[16,24,256]{2,1,0:T(8,128)(2,1)} %broadcast_in_dim.2), calls=%async_computation | async-start | bytes 393216 | tf_op jit(solution)/shard_map/all_to_all | solution.py:190
  10.7 0.1 pad_add_fusion.place_ref
  10.8 5.7 %build_mix.1.mix_ref = bf16[512,2304]{1,0:T(8,128)(2,1)S(1)} custom-call(s32[2]{0:T(128)S(1)} %pad_add_fusion.place_ref, s32[1,2]{1,0:T(1,128)} %hit_ref.1, s32[2,64,512]{2,1,0:T(8,128)} %bitcast.8, bf16[64,512]{1,0:T(8,128)(2,1)} %bitcast.9, s32[2,512]{1,0:T(2,128)} %bitcast.10), custom_call_target="tpu_custom_call" | custom-call | flops 536870912 | bytes 4194304 | tf_op jit(solution)/shard_map/build_mix/pallas_call | solution.py:103
  16.5 0.0 copy-start.1
  16.5 4.0 %all-to-all-done = bf16[16,24,256]{2,1,0:T(8,128)(2,1)S(1)} async-done(((bf16[16,24,256]{2,1,0:T(8,128)(2,1)}), bf16[16,24,256]{2,1,0:T(8,128)(2,1)S(1)}, u32[]{:S(2)}, u32[]{:S(2)}) %all-to-all-start) | async-done | bytes 196640 | tf_op jit(solution)/shard_map/all_to_all | solution.py:190
  20.4 0.0 collective-permute-start
  20.4 1.4 %collective-permute-done.other_ref = bf16[384,256]{1,0:T(8,128)(2,1)S(1)} collective-permute-done((bf16[384,256]{1,0:T(8,128)(2,1)S(1)}, bf16[384,256]{1,0:T(8,128)(2,1)S(1)}, u32[]{:S(2)}, u32[]{:S(2)}) %collective-permute-start) | collective-permute-done | bytes 196640 | tf_op jit(solution)/shard_map/ppermute | solution.py:186
  21.9 0.0 copy-done.2
  21.9 0.0 copy-done
  21.9 1.5 %sample.1 = bf16[8,64,256]{2,1,0:T(8,128)(2,1)S(1)} custom-call(s32[2]{0:T(128)S(1)} %pad_add_fusion.place_ref, s32[1,2]{1,0:T(1,128)S(1)} %copy-done.2, bf16[384,256]{1,0:T(8,128)(2,1)S(1)} %bitcast.7, bf16[384,256]{1,0:T(8,128)(2,1)S(1)} %collective-permute-done.other_ref, bf16[256,256]{1,0:T(8,128)(2,1)S(1)} %copy-done, ...), custom_call_target="tpu_custom_call" | custom-call | flops 536870912 | bytes 2097152 | tf_op jit(solution)/shard_map/sample/pallas_call | solution.py:154
  23.4 11.2 %all_to_all.10.pieces_ref = bf16[8,64,256]{2,1,0:T(8,128)(2,1)S(1)} all-to-all(bf16[8,64,256]{2,1,0:T(8,128)(2,1)S(1)} %sample.1), channel_id=1, replica_groups={{7,6,5,4,3,2,1,0},{15,14,13,12,11,10,9,8},{23,22,21,20,19,18,17,16},{31..., dimensions={0} | all-to-all | bytes 524288 | tf_op jit(solution)/shard_map/all_to_all | solution.py:190
  34.6 0.0 copy-done.1
  34.6 0.8 %project.1 = bf16[64,256]{1,0:T(8,128)(2,1)} custom-call(bf16[8,64,256]{2,1,0:T(8,128)(2,1)S(1)} %all_to_all.10.pieces_ref, bf16[256,256]{1,0:T(8,128)(2,1)S(1)} %copy-done.1), custom_call_target="tpu_custom_call" | custom-call | tf_op jit(solution)/shard_map/project/pallas_call | solution.py:175
Async XLA Ops:
  0.0 21.9 %copy-start.2 = (s32[1,2]{1,0:T(1,128)S(1)}, s32[1,2]{1,0:T(1,128)}, u32[]{:S(2)}) copy-start(s32[1,2]{1,0:T(1,128)} %hit_ref.1) | copy-start | bytes 28
  0.0 21.9 %copy-start = (bf16[256,256]{1,0:T(8,128)(2,1)S(1)}, bf16[256,256]{1,0:T(8,128)(2,1)}, u32[]{:S(2)}) copy-start(bf16[256,256]{1,0:T(8,128)(2,1)} %weight_ref.2) | copy-start | bytes 393220
  1.4 19.0 %all-to-all-start = ((bf16[16,24,256]{2,1,0:T(8,128)(2,1)}), bf16[16,24,256]{2,1,0:T(8,128)(2,1)S(1)}, u32[]{:S(2)}, u32[]{:S(2)}) async-start(bf16[16,24,256]{2,1,0:T(8,128)(2,1)} %broadcast_in_dim.2), calls=%async_computation | async-start | bytes 393216 | tf_op jit(solution)/shard_map/all_to_all | solution.py:190
  16.5 18.2 %copy-start.1 = (bf16[256,256]{1,0:T(8,128)(2,1)S(1)}, bf16[256,256]{1,0:T(8,128)(2,1)}, u32[]{:S(2)}) copy-start(bf16[256,256]{1,0:T(8,128)(2,1)} %weight_ref.3) | copy-start | bytes 393220
  20.4 1.4 %collective-permute-start = (bf16[384,256]{1,0:T(8,128)(2,1)S(1)}, bf16[384,256]{1,0:T(8,128)(2,1)S(1)}, u32[]{:S(2)}, u32[]{:S(2)}) collective-permute-start(bf16[384,256]{1,0:T(8,128)(2,1)S(1)} %bitcast.6), channel_id=1, source_target_pairs={{0,8},{8,0},{1,9},{9,1},{2,10},{10,2},{3,11},{11,3},{4,12},{12,4},... | collective-permute-start | bytes 589832 | tf_op jit(solution)/shard_map/ppermute | solution.py:186

commit v4 on v3

--- a/solution.py
+++ b/solution.py
@@ -18,9 +18,11 @@
 STRIPE = CAM_DEVICES * BLOCK
 STRIPES = 6
 WINDOW = STRIPES * BLOCK
+HALF_WINDOW = WINDOW // 2
 CHUNK = 16
 LANES = H * CHUNK
 CHUNKS = HITS * WINDOW // CHUNK
+HALF_CHUNKS = CHUNKS // 2
 Q_STEP = 32
 
 whole = pl.BlockSpec(memory_space=pltpu.VMEM)
@@ -33,7 +35,7 @@
 
 
 def mix_kernel(
-    place_ref, hit_any, index_any, attention_any, validity_any, mix_ref,
+    place_ref, hit_any, index_any, attention_any, validity_any, mix_ref, starts_ref,
     hit_ref, index_ref, attention_ref, validity_ref, row_ref, weight_ref, sems,
 ):
     copies = [
@@ -51,7 +53,7 @@
         copy.start()
     for copy in copies:
         copy.wait()
-    cam = place_ref[1]
+    core, cam = place_ref[0], place_ref[1]
     hit_count = validity_ref[0:1, :] + validity_ref[1:2, :]
     inverse = 1.0 / jnp.maximum(hit_count, 1).astype(jnp.float32)
     attention = attention_ref[...].astype(jnp.float32)
@@ -62,7 +64,9 @@
         stripe = (shifted * 683) >> 17
         within = shifted - stripe * STRIPE
         owner = (within * 171) >> 12
-        row = within - owner * BLOCK + stripe * BLOCK
+        row = within - owner * BLOCK + (STRIPES // 2 - 1 - (stripe >> 1)) * BLOCK
+        other = ((stripe + first_stripe(camera)) & 1) != core
+        row = jnp.where(other, row + HITS * HALF_WINDOW, row)
         row = jnp.where(owner == cam, row, -2 * CHUNK)
         rows.append(row.astype(jnp.float32))
         weights.append(attention * validity_ref[slot : slot + 1, :].astype(jnp.float32) * inverse)
@@ -78,33 +82,52 @@
             spread_weights = jnp.dot(weights, spread, preferred_element_type=jnp.float32)
             weight_ref[slot * K + k] = spread_weights.astype(jnp.bfloat16)
 
+    for half, parity in enumerate((core, 1 - core)):
+        for slot in range(HITS):
+            last = (first_stripe(hit_ref[0, slot]) + 1 - parity) // 2 + STRIPES // 2 - 1
+            line = half * HITS + slot
+            starts_ref[line : line + 1, :] = jnp.full((1, LANES), (ZY_DEVICES - 1 - last) * BLOCK, jnp.int32)
+
     local = lax.broadcasted_iota(jnp.int32, (Q_STEP, LANES), 1) % CHUNK
 
     @pl.loop(0, Q // Q_STEP)
     def _(step):
         part = pl.ds(pl.multiple_of(step * Q_STEP, Q_STEP), Q_STEP)
+        sums = {}
         for slot in range(HITS):
             picked = [row_ref[slot * K + k, part, :] for k in range(K)]
             scale = [weight_ref[slot * K + k, part, :] for k in range(K)]
             for chunk in slot_chunks(slot):
-                target = (local + (chunk * CHUNK - slot * WINDOW)).astype(jnp.int16)
-                total = jnp.zeros((Q_STEP, LANES), jnp.bfloat16)
+                target = (local + (chunk * CHUNK - slot * HALF_WINDOW)).astype(jnp.int16)
+                total = sums.pop(chunk, None)
+                if total is None:
+                    total = jnp.zeros((Q_STEP, LANES), jnp.bfloat16)
                 for k in range(K):
                     total = jnp.where(picked[k] == target, scale[k], total)
-                mix_ref[part, chunk * LANES : (chunk + 1) * LANES] = total
+                if slot == 0 and chunk in slot_chunks(1):
+                    sums[chunk] = total
+                else:
+                    mix_ref[part, chunk * LANES : (chunk + 1) * LANES] = total
 
 
 def slot_chunks(slot):
-    return range(slot * WINDOW // CHUNK, (slot + 1) * WINDOW // CHUNK)
+    found = []
+    for half in range(2):
+        first = (half * HITS + slot) * HALF_WINDOW
+        found += range(first // CHUNK, (first + HALF_WINDOW - 1) // CHUNK + 1)
+    return found
 
 
 def build_mix(place, hit_list, index, attention, validity):
     inputs = (pltpu.with_memory_space_constraint(x, pltpu.HBM) for x in (hit_list, index, attention, validity))
     return pl.pallas_call(
         mix_kernel,
-        out_shape=jax.ShapeDtypeStruct((Q, CHUNKS * LANES), jnp.bfloat16),
+        out_shape=(
+            jax.ShapeDtypeStruct((Q, CHUNKS * LANES), jnp.bfloat16),
+            jax.ShapeDtypeStruct((2 * HITS, LANES), jnp.int32),
+        ),
         in_specs=[scalars, anywhere, anywhere, anywhere, anywhere],
-        out_specs=whole,
+        out_specs=(whole, whole),
         scratch_shapes=[
             pltpu.SMEM((1, HITS), jnp.int32),
             pltpu.VMEM((HITS, H * K, Q), jnp.int32),
@@ -120,45 +143,47 @@
     )(place, *inputs)
 
 
-def sample_kernel(place_ref, hit_ref, mine_ref, other_ref, weight_ref, mix_ref, out_ref):
-    core = place_ref[0]
-    blocks = []
+def mixed(starts_ref, gathered_ref, half, weight_ref, mix, spread_ref):
+    windows = []
     for slot in range(HITS):
-        first = first_stripe(hit_ref[0, slot])
-        for i in range(STRIPES):
-            tile = first + i
-            part = pl.ds(pl.multiple_of((ZY_DEVICES - 1 - (tile >> 1)) * BLOCK, 8), BLOCK)
-            blocks.append(jnp.where((tile & 1) == core, mine_ref[part, :], other_ref[part, :]))
-    features = jnp.concatenate(blocks, axis=0)
-    values = jnp.dot(features, weight_ref[...], preferred_element_type=jnp.float32)
+        start = pl.multiple_of(starts_ref[half * HITS + slot, 0], 8)
+        windows.append(gathered_ref[pl.ds(start, HALF_WINDOW), :])
+    features = jnp.concatenate(windows, axis=0)
+    values = jnp.dot(features, weight_ref[...], preferred_element_type=jnp.float32).astype(jnp.bfloat16)
     head_of_row = lax.broadcasted_iota(jnp.int32, (LANES, D), 0) // CHUNK
     head_of_column = lax.broadcasted_iota(jnp.int32, (LANES, D), 1) // (D // H)
     same_head = head_of_row == head_of_column
-    total = jnp.zeros((Q, D), jnp.float32)
-    for pair in range(CHUNKS // 2):
-        blocks = []
-        for chunk in (2 * pair, 2 * pair + 1):
-            piece = values[chunk * CHUNK : (chunk + 1) * CHUNK, :]
-            tall = jnp.concatenate([piece] * H, axis=0)
-            blocks.append(jnp.where(same_head, tall, 0.0).astype(jnp.bfloat16))
-        block = jnp.concatenate(blocks, axis=0)
-        columns = slice(2 * pair * LANES, (2 * pair + 2) * LANES)
-        total = total + jnp.dot(mix_ref[:, columns], block, preferred_element_type=jnp.float32)
+    for chunk in range(HALF_CHUNKS):
+        piece = values[chunk * CHUNK : (chunk + 1) * CHUNK, :]
+        tall = jnp.concatenate([piece] * H, axis=0)
+        spread_ref[chunk * LANES : (chunk + 1) * LANES, :] = jnp.where(same_head, tall, jnp.zeros((), jnp.bfloat16))
+    return jnp.dot(mix, spread_ref[...], preferred_element_type=jnp.float32)
+
+
+def near_kernel(starts_ref, mine_ref, weight_ref, mix_ref, out_ref, spread_ref):
+    out_ref[...] = mixed(starts_ref, mine_ref, 0, weight_ref, mix_ref[:, : HALF_CHUNKS * LANES], spread_ref)
+
+
+def far_kernel(starts_ref, other_ref, weight_ref, mix_ref, near_ref, out_ref, spread_ref):
+    total = near_ref[...] + mixed(
+        starts_ref, other_ref, 1, weight_ref, mix_ref[:, HALF_CHUNKS * LANES :], spread_ref
+    )
     total = total.astype(jnp.bfloat16)
     share = Q // CAM_DEVICES
     for i in range(CAM_DEVICES):
         out_ref[CAM_DEVICES - 1 - i] = total[i * share : (i + 1) * share, :]
 
 
-def sample(*operands):
+def sample(kernel, name, out_shape, *operands):
     return pl.pallas_call(
-        sample_kernel,
-        out_shape=jax.ShapeDtypeStruct((CAM_DEVICES, Q // CAM_DEVICES, D), jnp.bfloat16),
-        in_specs=[scalars, scalars, whole, whole, whole, whole],
+        kernel,
+        out_shape=out_shape,
+        in_specs=[whole] * len(operands),
         out_specs=whole,
+        scratch_shapes=[pltpu.VMEM((HALF_CHUNKS * LANES, D), jnp.bfloat16)],
         compiler_params=pltpu.CompilerParams(vmem_limit_bytes=16 << 20),
-        cost_estimate=pl.CostEstimate(flops=1 << 29, bytes_accessed=2 << 20, transcendentals=0),
-        name="sample",
+        cost_estimate=pl.CostEstimate(flops=1 << 28, bytes_accessed=1 << 20, transcendentals=0),
+        name=name,
     )(*operands)
 
 
@@ -194,10 +219,13 @@
     place = jnp.stack([lax.axis_index("core"), lax.axis_index("cam")]).astype(jnp.int32)
     copies = jnp.broadcast_to(features[None], (ZY_DEVICES, BLOCK, D))
     mine = exchanged(copies, "zy", list(reversed(range(ZY_DEVICES)))).reshape(ZY_DEVICES * BLOCK, D)
-    mix = build_mix(place, hit_list, sample_index.transpose(1, 2, 0), attention.T, validity.T)
-    mine, mix = lax.optimization_barrier((mine, mix))
+    mix, starts = build_mix(place, hit_list, sample_index.transpose(1, 2, 0), attention.T, validity.T)
+    mine, mix, starts = lax.optimization_barrier((mine, mix, starts))
     other = swapped(mine, "core")
-    pieces = sample(place, hit_list, mine, other, value_weight, mix)
+    near_shape = jax.ShapeDtypeStruct((Q, D), jnp.float32)
+    near = sample(near_kernel, "sample_near", near_shape, starts, mine, value_weight, mix)
+    pieces_shape = jax.ShapeDtypeStruct((CAM_DEVICES, Q // CAM_DEVICES, D), jnp.bfloat16)
+    pieces = sample(far_kernel, "sample_far", pieces_shape, starts, other, value_weight, mix, near)
     arrived = exchanged(pieces, "cam", list(reversed(range(CAM_DEVICES))))
     return project(arrived, output_weight)
 

time: 35.7 us -> 34.9 us (0.978)
  waiting for transfers between devices: 5.41 us -> 4.16 us
  Pallas kernels: 8.01 us -> 8.42 us
    ppermute x1, waiting for transfers between devices: 1.44 us -> 0.72 us  [swapped(): return lax.ppermute(x, axis, [(0, 1), (1, 0)])]
    all_to_all x1, waiting for transfers between devices: 3.97 us -> 3.43 us  [exchanged(): return lax.all_to_all(x, axis, 0, 0, tiled=True, axis_index_groups=[order])]
    pallas_call x2 -> x3, Pallas kernels: 7.23 us -> 7.63 us  [the longest x1 6.24 us: build_mix(): pl.pallas_call(mix_kernel, out_shape=(jax.ShapeDtypeStruct((Q, CHUNKS * L...]
  transfers between devices with their start and end apart: 2 -> 2, of which waited for: 2 -> 2; matrix products, arithmetic and copies ran while one was open for 0% -> 0% of each run, Pallas kernels for 16% -> 20%
where the time goes in v4:
time: 34.9 us; the launch traced here: 34.6 us
  blocking collectives  11.2 us (32%)
  starting transfers between devices  9.26 us (27%)
  Pallas kernels  8.42 us (24%)
  waiting for transfers between devices  4.16 us (12%)
  local copies, waits for them, and re-layouts  1.43 us (4%)
    all_to_all x1, blocking collectives, exchanged(): return lax.all_to_all(x, axis, 0, 0, tiled=True, axis_index_groups=[order])  11.2 us
    all_to_all x1, starting transfers between devices, exchanged(): return lax.all_to_all(x, axis, 0, 0, tiled=True, axis_index_groups=[order])  9.25 us
    pallas_call x1, Pallas kernels, build_mix(): pl.pallas_call(mix_kernel, out_shape=(jax.ShapeDtypeStruct((Q, CHUNKS * L...  6.24 us
    all_to_all x1, waiting for transfers between devices, exchanged(): return lax.all_to_all(x, axis, 0, 0, tiled=True, axis_index_groups=[order])  3.43 us
    broadcast_in_dim x1, local copies, waits for them, and re-layouts, body(): copies = jnp.broadcast_to(features[None], (ZY_DEVICES, BLOCK, D))  1.42 us
    pallas_call x2, Pallas kernels, sample(): pl.pallas_call(kernel, out_shape=out_shape, in_specs=[whole] * len(operan...  1.39 us
    pallas_call x1, Pallas kernels, project(): pl.pallas_call(project_kernel, out_shape=jax.ShapeDtypeStruct((Q // CAM_D...  0.78 us
    ppermute x1, waiting for transfers between devices, swapped(): return lax.ppermute(x, axis, [(0, 1), (1, 0)])  0.72 us
  transfers between devices with their start and end apart: 2, of which 2 were waited for; matrix products, arithmetic and copies ran while one was open for 0% of the time, Pallas kernels for 20%

profile of v4, /device:TPU:16, one launch (start us, length us, event | category | flops | bytes accessed | tf_op | source)
XLA Modules:
  0.0 34.6 jit_solution(8370003651513429833)
XLA Ops:
  0.0 0.0 copy-start
  0.0 1.4 %broadcast_in_dim.2 = bf16[16,24,256]{2,1,0:T(8,128)(2,1)} broadcast(bf16[24,256]{1,0:T(8,128)(2,1)} %param.7), dimensions={1,2} | broadcast | bytes 208896 | tf_op jit(solution)/shard_map/broadcast_in_dim | solution.py:220
  1.4 9.3 %all-to-all-start = ((bf16[16,24,256]{2,1,0:T(8,128)(2,1)}), bf16[16,24,256]{2,1,0:T(8,128)(2,1)S(1)}, u32[]{:S(2)}, u32[]{:S(2)}) async-start(bf16[16,24,256]{2,1,0:T(8,128)(2,1)} %broadcast_in_dim.2), calls=%async_computation | async-start | bytes 393216 | tf_op jit(solution)/shard_map/all_to_all | solution.py:215
  10.7 0.1 pad_add_fusion.place_ref
  10.8 6.2 %build_mix.1 = (bf16[512,2304]{1,0:T(8,128)(2,1)S(1)}, s32[4,128]{1,0:T(4,128)S(1)}) custom-call(s32[2]{0:T(128)S(1)} %pad_add_fusion.place_ref, s32[1,2]{1,0:T(1,128)} %hit_any.1, s32[2,64,512]{2,1,0:T(8,128)} %bitcast.8, bf16[64,512]{1,0:T(8,128)(2,1)} %bitcast.9, s32[2,512]{1,0:T(2,128)} %bitcast.10), custom_call_target="tpu_custom_call" | custom-call | flops 536870912 | bytes 4194304 | tf_op jit(solution)/shard_map/build_mix/pallas_call | solution.py:123
  17.0 3.4 %all-to-all-done = bf16[16,24,256]{2,1,0:T(8,128)(2,1)S(1)} async-done(((bf16[16,24,256]{2,1,0:T(8,128)(2,1)}), bf16[16,24,256]{2,1,0:T(8,128)(2,1)S(1)}, u32[]{:S(2)}, u32[]{:S(2)}) %all-to-all-start) | async-done | bytes 196640 | tf_op jit(solution)/shard_map/all_to_all | solution.py:215
  20.4 0.0 collective-permute-start
  20.4 0.0 copy-done
  20.4 0.7 %sample_near.1.near_ref = f32[512,256]{1,0:T(8,128)S(1)} custom-call(s32[4,128]{1,0:T(4,128)S(1)} %get-tuple-element.12.starts_ref, bf16[384,256]{1,0:T(8,128)(2,1)S(1)} %bitcast.7, bf16[256,256]{1,0:T(8,128)(2,1)S(1)} %copy-done, bf16[512,2304]{1,0:T(8,128)(2,1)S(1)} %get-tuple-element.14.mix_ref), custom_call_target="tpu_custom_call" | custom-call | flops 268435456 | bytes 1048576 | tf_op jit(solution)/shard_map/sample_near/pallas_call | solution.py:178
  21.1 0.0 copy-start.1
  21.2 0.7 %collective-permute-done.other_ref = bf16[384,256]{1,0:T(8,128)(2,1)S(1)} collective-permute-done((bf16[384,256]{1,0:T(8,128)(2,1)S(1)}, bf16[384,256]{1,0:T(8,128)(2,1)S(1)}, u32[]{:S(2)}, u32[]{:S(2)}) %collective-permute-start) | collective-permute-done | bytes 196640 | tf_op jit(solution)/shard_map/ppermute | solution.py:211
  21.9 0.7 %sample_far.1 = bf16[8,64,256]{2,1,0:T(8,128)(2,1)S(1)} custom-call(s32[4,128]{1,0:T(4,128)S(1)} %get-tuple-element.12.starts_ref, bf16[384,256]{1,0:T(8,128)(2,1)S(1)} %collective-permute-done.other_ref, bf16[256,256]{1,0:T(8,128)(2,1)S(1)} %copy-done, bf16[512,2304]{1,0:T(8,128)(2,1)S(1)} %get-tuple-element.14.mix_ref, f32[512,256]{1,0:T(8,128)S(1)} %sample_near.1.near_ref), custom_call_target="tpu_custom_call" | custom-call | flops 268435456 | bytes 1048576 | tf_op jit(solution)/shard_map/sample_far/pallas_call | solution.py:178
  22.6 11.2 %all_to_all.10.pieces_ref = bf16[8,64,256]{2,1,0:T(8,128)(2,1)S(1)} all-to-all(bf16[8,64,256]{2,1,0:T(8,128)(2,1)S(1)} %sample_far.1), channel_id=1, replica_groups={{7,6,5,4,3,2,1,0},{15,14,13,12,11,10,9,8},{23,22,21,20,19,18,17,16},{31..., dimensions={0} | all-to-all | bytes 524288 | tf_op jit(solution)/shard_map/all_to_all | solution.py:215
  33.8 0.0 copy-done.1
  33.8 0.8 %project.1 = bf16[64,256]{1,0:T(8,128)(2,1)} custom-call(bf16[8,64,256]{2,1,0:T(8,128)(2,1)S(1)} %all_to_all.10.pieces_ref, bf16[256,256]{1,0:T(8,128)(2,1)S(1)} %copy-done.1), custom_call_target="tpu_custom_call" | custom-call | tf_op jit(solution)/shard_map/project/pallas_call | solution.py:200
Async XLA Ops:
  0.0 20.4 %copy-start = (bf16[256,256]{1,0:T(8,128)(2,1)S(1)}, bf16[256,256]{1,0:T(8,128)(2,1)}, u32[]{:S(2)}) copy-start(bf16[256,256]{1,0:T(8,128)(2,1)} %weight_ref.4) | copy-start | bytes 393220
  1.4 19.0 %all-to-all-start = ((bf16[16,24,256]{2,1,0:T(8,128)(2,1)}), bf16[16,24,256]{2,1,0:T(8,128)(2,1)S(1)}, u32[]{:S(2)}, u32[]{:S(2)}) async-start(bf16[16,24,256]{2,1,0:T(8,128)(2,1)} %broadcast_in_dim.2), calls=%async_computation | async-start | bytes 393216 | tf_op jit(solution)/shard_map/all_to_all | solution.py:215
  20.4 1.4 %collective-permute-start = (bf16[384,256]{1,0:T(8,128)(2,1)S(1)}, bf16[384,256]{1,0:T(8,128)(2,1)S(1)}, u32[]{:S(2)}, u32[]{:S(2)}) collective-permute-start(bf16[384,256]{1,0:T(8,128)(2,1)S(1)} %bitcast.6), channel_id=1, source_target_pairs={{0,8},{8,0},{1,9},{9,1},{2,10},{10,2},{3,11},{11,3},{4,12},{12,4},... | collective-permute-start | bytes 589832 | tf_op jit(solution)/shard_map/ppermute | solution.py:211
  21.1 12.6 %copy-start.1 = (bf16[256,256]{1,0:T(8,128)(2,1)S(1)}, bf16[256,256]{1,0:T(8,128)(2,1)}, u32[]{:S(2)}) copy-start(bf16[256,256]{1,0:T(8,128)(2,1)} %weight_ref.5) | copy-start | bytes 393220

commit v5 on v4

v5 whole, which is shorter than its diff:
```python
import jax
import jax.numpy as jnp
from jax import lax
from jax.experimental import pallas as pl
from jax.experimental.pallas import tpu as pltpu
from jax.sharding import Mesh, PartitionSpec as P

D = 256
H = 8
K = 8
HITS = 2
CAM_ROWS = 1024
Q = 512
CAM_DEVICES = 8
ZY_DEVICES = 16

BLOCK = 24
STRIPE = CAM_DEVICES * BLOCK
STRIPES = 6
WINDOW = STRIPES * BLOCK
HALF_WINDOW = WINDOW // 2
CHUNK = 8
LANES = HITS * H * CHUNK
CHUNKS = WINDOW // CHUNK
HALF_CHUNKS = CHUNKS // 2
Q_STEP = 32

whole = pl.BlockSpec(memory_space=pltpu.VMEM)
anywhere = pl.BlockSpec(memory_space=pltpu.HBM)


def listed(i):
    return i ^ 9


def first_stripe(camera):
    return (camera * 16) // 3


def mix_kernel(
    hit_any, index_any, attention_any, validity_any, mix_ref, starts_ref,
    hit_ref, index_ref, attention_ref, validity_ref, row_ref, weight_ref, sems,
):
    copies = [
        pltpu.make_async_copy(source, target, sems.at[i])
        for i, (source, target) in enumerate(
            (
                (index_any, index_ref),
                (attention_any, attention_ref),
                (validity_any, validity_ref),
                (hit_any, hit_ref),
            )
        )
    ]
    for copy in copies:
        copy.start()
    for copy in copies:
        copy.wait()
    core, cam = lax.axis_index("core"), lax.axis_index("cam")
    hit_count = validity_ref[0:1, :] + validity_ref[1:2, :]
    inverse = 1.0 / jnp.maximum(hit_count, 1).astype(jnp.float32)
    attention = attention_ref[...].astype(jnp.float32)
    rows, weights = [], []
    for slot in range(HITS):
        camera = hit_ref[0, slot]
        shifted = index_ref[slot] + (camera * CAM_ROWS - first_stripe(camera) * STRIPE)
        stripe = (shifted * 683) >> 17
        within = shifted - stripe * STRIPE
        owner = (within * 171) >> 12
        row = within - owner * BLOCK + (stripe >> 1) * BLOCK
        other = ((stripe + first_stripe(camera)) & 1) != core
        row = jnp.where(other, row + HALF_WINDOW, row)
        row = jnp.where(owner == cam, row, -1)
        rows.append(row.astype(jnp.float32))
        weights.append(attention * validity_ref[slot : slot + 1, :].astype(jnp.float32) * inverse)
    rows = jnp.concatenate(rows, axis=0).T.astype(jnp.bfloat16)
    weights = jnp.concatenate(weights, axis=0).T.astype(jnp.bfloat16)
    source = lax.broadcasted_iota(jnp.int32, (HITS * H * K, LANES), 0)
    group = lax.broadcasted_iota(jnp.int32, (HITS * H * K, LANES), 1) // CHUNK
    for k in range(K):
        spread = (source == group * K + k).astype(jnp.bfloat16)
        spread_rows = jnp.dot(rows, spread, preferred_element_type=jnp.float32)
        row_ref[k] = spread_rows.astype(jnp.int32).astype(jnp.int16)
        spread_weights = jnp.dot(weights, spread, preferred_element_type=jnp.float32)
        weight_ref[k] = spread_weights.astype(jnp.bfloat16)

    for half, parity in enumerate((core, 1 - core)):
        for slot in range(HITS):
            first = (first_stripe(hit_ref[0, slot]) + 1 - parity) // 2
            for i in range(STRIPES // 2):
                line = (half * HITS + slot) * (STRIPES // 2) + i
                starts_ref[line : line + 1, :] = jnp.full((1, LANES), listed(first + i) * BLOCK, jnp.int32)

    local = lax.broadcasted_iota(jnp.int32, (Q_STEP, LANES), 1) % CHUNK

    @pl.loop(0, Q // Q_STEP)
    def _(step):
        part = pl.ds(pl.multiple_of(step * Q_STEP, Q_STEP), Q_STEP)
        picked = [row_ref[k, part, :] for k in range(K)]
        scale = [weight_ref[k, part, :] for k in range(K)]
        for chunk in range(CHUNKS):
            target = (local + chunk * CHUNK).astype(jnp.int16)
            total = jnp.zeros((Q_STEP, LANES), jnp.bfloat16)
            for k in range(K):
                total = jnp.where(picked[k] == target, scale[k], total)
            mix_ref[part, chunk * LANES : (chunk + 1) * LANES] = total.astype(jnp.bfloat16)


def build_mix(hit_list, index, attention, validity):
    inputs = (pltpu.with_memory_space_constraint(x, pltpu.HBM) for x in (hit_list, index, attention, validity))
    return pl.pallas_call(
        mix_kernel,
        out_shape=(
            jax.ShapeDtypeStruct((Q, CHUNKS * LANES), jnp.bfloat16),
            jax.ShapeDtypeStruct((HITS * STRIPES, LANES), jnp.int32),
        ),
        in_specs=[anywhere, anywhere, anywhere, anywhere],
        out_specs=(whole, whole),
        scratch_shapes=[
            pltpu.SMEM((1, HITS), jnp.int32),
            pltpu.VMEM((HITS, H * K, Q), jnp.int32),
            pltpu.VMEM((H * K, Q), jnp.bfloat16),
            pltpu.VMEM((HITS, Q), jnp.int32),
            pltpu.VMEM((K, Q, LANES), jnp.int16),
            pltpu.VMEM((K, Q, LANES), jnp.bfloat16),
            pltpu.SemaphoreType.DMA((4,)),
        ],
        compiler_params=pltpu.CompilerParams(vmem_limit_bytes=16 << 20),
        cost_estimate=pl.CostEstimate(flops=1 << 29, bytes_accessed=4 << 20, transcendentals=0),
        name="build_mix",
    )(*inputs)


def mixed(starts_ref, gathered_ref, half, weight_ref, mix, spread_ref):
    windows = []
    for slot in range(HITS):
        for i in range(STRIPES // 2):
            start = pl.multiple_of(starts_ref[(half * HITS + slot) * (STRIPES // 2) + i, 0], 8)
            windows.append(gathered_ref[pl.ds(start, BLOCK), :])
    features = jnp.concatenate(windows, axis=0)
    values = jnp.dot(features, weight_ref[...], preferred_element_type=jnp.float32)
    head_of_row = (lax.broadcasted_iota(jnp.int32, (LANES, D), 0) // CHUNK) % H
    head_of_column = lax.broadcasted_iota(jnp.int32, (LANES, D), 1) // (D // H)
    same_head = head_of_row == head_of_column
    for chunk in range(HALF_CHUNKS):
        pieces = []
        for slot in range(HITS):
            first = slot * HALF_WINDOW + chunk * CHUNK
            pieces += [values[first : first + CHUNK, :]] * H
        tall = jnp.where(same_head, jnp.concatenate(pieces, axis=0), 0.0)
        spread_ref[chunk * LANES : (chunk + 1) * LANES, :] = tall.astype(jnp.bfloat16)
    return jnp.dot(mix, spread_ref[...], preferred_element_type=jnp.float32)


def near_kernel(starts_ref, mine_ref, weight_ref, mix_ref, out_ref, spread_ref):
    out_ref[...] = mixed(starts_ref, mine_ref, 0, weight_ref, mix_ref[:, : HALF_CHUNKS * LANES], spread_ref)


def far_kernel(starts_ref, other_ref, weight_ref, mix_ref, near_ref, out_ref, spread_ref):
    total = near_ref[...] + mixed(
        starts_ref, other_ref, 1, weight_ref, mix_ref[:, HALF_CHUNKS * LANES :], spread_ref
    )
    total = total.astype(jnp.bfloat16)
    share = Q // CAM_DEVICES
    for i in range(CAM_DEVICES):
        out_ref[CAM_DEVICES - 1 - i] = total[i * share : (i + 1) * share, :]


def sample(kernel, name, out_shape, *operands):
    return pl.pallas_call(
        kernel,
        out_shape=out_shape,
        in_specs=[whole] * len(operands),
        out_specs=whole,
        scratch_shapes=[pltpu.VMEM((HALF_CHUNKS * LANES, D), jnp.bfloat16)],
        compiler_params=pltpu.CompilerParams(vmem_limit_bytes=16 << 20),
        cost_estimate=pl.CostEstimate(flops=1 << 28, bytes_accessed=1 << 20, transcendentals=0),
        name=name,
    )(*operands)


def project_kernel(pieces_ref, weight_ref, out_ref):
    total = pieces_ref[0].astype(jnp.float32)
    for i in range(1, CAM_DEVICES):
        total = total + pieces_ref[i].astype(jnp.float32)
    out_ref[...] = jnp.dot(
        total.astype(jnp.bfloat16), weight_ref[...], preferred_element_type=jnp.float32
    ).astype(jnp.bfloat16)


def project(pieces, output_weight):
    return pl.pallas_call(
        project_kernel,
        out_shape=jax.ShapeDtypeStruct((Q // CAM_DEVICES, D), jnp.bfloat16),
        in_specs=[whole, whole],
        out_specs=whole,
        compiler_params=pltpu.CompilerParams(vmem_limit_bytes=8 << 20),
        name="project",
    )(pieces, output_weight)


def swapped(x, axis):
    return lax.ppermute(x, axis, [(0, 1), (1, 0)])


def exchanged(x, axis, order):
    return lax.all_to_all(x, axis, 0, 0, tiled=True, axis_index_groups=[order])


def body(features, value_weight, output_weight, hit_list, sample_index, attention, validity):
    copies = jnp.broadcast_to(features[None], (ZY_DEVICES, BLOCK, D))
    mine = exchanged(copies, "zy", [listed(i) for i in range(ZY_DEVICES)]).reshape(ZY_DEVICES * BLOCK, D)
    mix, starts = build_mix(hit_list, sample_index.transpose(1, 2, 0), attention.T, validity.T)
    mine, mix, starts = lax.optimization_barrier((mine, mix, starts))
    other = swapped(mine, "core")
    near_shape = jax.ShapeDtypeStruct((Q, D), jnp.float32)
    near = sample(near_kernel, "sample_near", near_shape, starts, mine, value_weight, mix)
    pieces_shape = jax.ShapeDtypeStruct((CAM_DEVICES, Q // CAM_DEVICES, D), jnp.bfloat16)
    pieces = sample(far_kernel, "sample_far", pieces_shape, starts, other, value_weight, mix, near)
    arrived = exchanged(pieces, "cam", list(reversed(range(CAM_DEVICES))))
    return project(arrived, output_weight)


def solution(mesh):
    split = Mesh(mesh.devices.reshape(ZY_DEVICES, 2, CAM_DEVICES), ("zy", "core", "cam"))
    tile = ("zy", "core")
    every = tile + ("cam",)
    in_specs = (
        P(every, None),
        P(),
        P(),
        P(tile, None),
        P(tile, None, None),
        P(tile, None),
        P(tile, None),
    )
    return jax.shard_map(body, mesh=split, in_specs=in_specs, out_specs=P(every, None), check_vma=False)
```

time: 34.9 us -> 34.3 us (0.983)
  Pallas kernels: 8.42 us -> 6.88 us
  starting transfers between devices: 9.26 us -> 10.5 us
    pallas_call x1, Pallas kernels: 6.24 us -> 4.7 us  [build_mix(): pl.pallas_call(mix_kernel, out_shape=(jax.ShapeDtypeStruct((Q, CHUNKS * L...]
    all_to_all x1, starting transfers between devices: 9.25 us -> 10.5 us  [exchanged(): return lax.all_to_all(x, axis, 0, 0, tiled=True, axis_index_groups=[order])]
  transfers between devices with their start and end apart: 2 -> 2, of which waited for: 2 -> 2; matrix products, arithmetic and copies ran while one was open for 0% -> 0% of each run, Pallas kernels for 20% -> 16%
where the time goes in v5:
time: 34.3 us; the launch traced here: 34 us
  blocking collectives  11.3 us (33%)
  starting transfers between devices  10.5 us (31%)
  Pallas kernels  6.88 us (20%)
  waiting for transfers between devices  3.82 us (11%)
  local copies, waits for them, and re-layouts  1.43 us (4%)
    all_to_all x1, blocking collectives, exchanged(): return lax.all_to_all(x, axis, 0, 0, tiled=True, axis_index_groups=[order])  11.3 us
    all_to_all x1, starting transfers between devices, exchanged(): return lax.all_to_all(x, axis, 0, 0, tiled=True, axis_index_groups=[order])  10.5 us
    pallas_call x1, Pallas kernels, build_mix(): pl.pallas_call(mix_kernel, out_shape=(jax.ShapeDtypeStruct((Q, CHUNKS * L...  4.7 us
    all_to_all x1, waiting for transfers between devices, exchanged(): return lax.all_to_all(x, axis, 0, 0, tiled=True, axis_index_groups=[order])  3.1 us
    broadcast_in_dim x1, local copies, waits for them, and re-layouts, body(): copies = jnp.broadcast_to(features[None], (ZY_DEVICES, BLOCK, D))  1.42 us
    pallas_call x2, Pallas kernels, sample(): pl.pallas_call(kernel, out_shape=out_shape, in_specs=[whole] * len(operan...  1.4 us
    pallas_call x1, Pallas kernels, project(): pl.pallas_call(project_kernel, out_shape=jax.ShapeDtypeStruct((Q // CAM_D...  0.78 us
    ppermute x1, waiting for transfers between devices, swapped(): return lax.ppermute(x, axis, [(0, 1), (1, 0)])  0.72 us
  transfers between devices with their start and end apart: 2, of which 2 were waited for; matrix products, arithmetic and copies ran while one was open for 0% of the time, Pallas kernels for 16%

profile of v5, /device:TPU:16, one launch (start us, length us, event | category | flops | bytes accessed | tf_op | source)
XLA Modules:
  0.0 34.0 jit_solution(17089008707395470714)
XLA Ops:
  0.0 0.0 copy-start
  0.0 1.4 %broadcast_in_dim.2 = bf16[16,24,256]{2,1,0:T(8,128)(2,1)} broadcast(bf16[24,256]{1,0:T(8,128)(2,1)} %param.7), dimensions={1,2} | broadcast | bytes 208896 | tf_op jit(solution)/shard_map/broadcast_in_dim | solution.py:211
  1.4 10.5 %all-to-all-start = ((bf16[16,24,256]{2,1,0:T(8,128)(2,1)}), bf16[16,24,256]{2,1,0:T(8,128)(2,1)S(1)}, u32[]{:S(2)}, u32[]{:S(2)}) async-start(bf16[16,24,256]{2,1,0:T(8,128)(2,1)} %broadcast_in_dim.2), calls=%async_computation | async-start | bytes 393216 | tf_op jit(solution)/shard_map/all_to_all | solution.py:207
  12.0 4.7 %build_mix.1 = (bf16[512,2304]{1,0:T(8,128)(2,1)S(1)}, s32[12,128]{1,0:T(8,128)S(1)}) custom-call(s32[1,2]{1,0:T(1,128)} %hit_any.1, s32[2,64,512]{2,1,0:T(8,128)} %bitcast.6, bf16[64,512]{1,0:T(8,128)(2,1)} %bitcast.7, s32[2,512]{1,0:T(2,128)} %bitcast.8), custom_call_target="tpu_custom_call" | custom-call | flops 536870912 | bytes 4194304 | tf_op jit(solution)/shard_map/build_mix/pallas_call | solution.py:111
  16.7 3.1 %all-to-all-done = bf16[16,24,256]{2,1,0:T(8,128)(2,1)S(1)} async-done(((bf16[16,24,256]{2,1,0:T(8,128)(2,1)}), bf16[16,24,256]{2,1,0:T(8,128)(2,1)S(1)}, u32[]{:S(2)}, u32[]{:S(2)}) %all-to-all-start) | async-done | bytes 196640 | tf_op jit(solution)/shard_map/all_to_all | solution.py:207
  19.8 0.0 collective-permute-start
  19.8 0.0 copy-done
  19.8 0.7 %sample_near.1.near_ref = f32[512,256]{1,0:T(8,128)S(1)} custom-call(s32[12,128]{1,0:T(8,128)S(1)} %get-tuple-element.12.starts_ref, bf16[384,256]{1,0:T(8,128)(2,1)S(1)} %bitcast.5, bf16[256,256]{1,0:T(8,128)(2,1)S(1)} %copy-done, bf16[512,2304]{1,0:T(8,128)(2,1)S(1)} %get-tuple-element.14.mix_ref), custom_call_target="tpu_custom_call" | custom-call | flops 268435456 | bytes 1048576 | tf_op jit(solution)/shard_map/sample_near/pallas_call | solution.py:170
  20.5 0.0 copy-start.1
  20.5 0.7 %collective-permute-done.other_ref = bf16[384,256]{1,0:T(8,128)(2,1)S(1)} collective-permute-done((bf16[384,256]{1,0:T(8,128)(2,1)S(1)}, bf16[384,256]{1,0:T(8,128)(2,1)S(1)}, u32[]{:S(2)}, u32[]{:S(2)}) %collective-permute-start) | collective-permute-done | bytes 196640 | tf_op jit(solution)/shard_map/ppermute | solution.py:203
  21.2 0.7 %sample_far.1 = bf16[8,64,256]{2,1,0:T(8,128)(2,1)S(1)} custom-call(s32[12,128]{1,0:T(8,128)S(1)} %get-tuple-element.12.starts_ref, bf16[384,256]{1,0:T(8,128)(2,1)S(1)} %collective-permute-done.other_ref, bf16[256,256]{1,0:T(8,128)(2,1)S(1)} %copy-done, bf16[512,2304]{1,0:T(8,128)(2,1)S(1)} %get-tuple-element.14.mix_ref, f32[512,256]{1,0:T(8,128)S(1)} %sample_near.1.near_ref), custom_call_target="tpu_custom_call" | custom-call | flops 268435456 | bytes 1048576 | tf_op jit(solution)/shard_map/sample_far/pallas_call | solution.py:170
  21.9 11.3 %all_to_all.10.pieces_ref = bf16[8,64,256]{2,1,0:T(8,128)(2,1)S(1)} all-to-all(bf16[8,64,256]{2,1,0:T(8,128)(2,1)S(1)} %sample_far.1), channel_id=1, replica_groups={{7,6,5,4,3,2,1,0},{15,14,13,12,11,10,9,8},{23,22,21,20,19,18,17,16},{31..., dimensions={0} | all-to-all | bytes 524288 | tf_op jit(solution)/shard_map/all_to_all | solution.py:207
  33.2 0.0 copy-done.1
  33.2 0.8 %project.1 = bf16[64,256]{1,0:T(8,128)(2,1)} custom-call(bf16[8,64,256]{2,1,0:T(8,128)(2,1)S(1)} %all_to_all.10.pieces_ref, bf16[256,256]{1,0:T(8,128)(2,1)S(1)} %copy-done.1), custom_call_target="tpu_custom_call" | custom-call | tf_op jit(solution)/shard_map/project/pallas_call | solution.py:192
Async XLA Ops:
  0.0 19.8 %copy-start = (bf16[256,256]{1,0:T(8,128)(2,1)S(1)}, bf16[256,256]{1,0:T(8,128)(2,1)}, u32[]{:S(2)}) copy-start(bf16[256,256]{1,0:T(8,128)(2,1)} %weight_ref.4) | copy-start | bytes 393220
  1.4 18.4 %all-to-all-start = ((bf16[16,24,256]{2,1,0:T(8,128)(2,1)}), bf16[16,24,256]{2,1,0:T(8,128)(2,1)S(1)}, u32[]{:S(2)}, u32[]{:S(2)}) async-start(bf16[16,24,256]{2,1,0:T(8,128)(2,1)} %broadcast_in_dim.2), calls=%async_computation | async-start | bytes 393216 | tf_op jit(solution)/shard_map/all_to_all | solution.py:207
  19.8 1.4 %collective-permute-start = (bf16[384,256]{1,0:T(8,128)(2,1)S(1)}, bf16[384,256]{1,0:T(8,128)(2,1)S(1)}, u32[]{:S(2)}, u32[]{:S(2)}) collective-permute-start(bf16[384,256]{1,0:T(8,128)(2,1)S(1)} %bitcast.4), channel_id=1, source_target_pairs={{0,8},{8,0},{1,9},{9,1},{2,10},{10,2},{3,11},{11,3},{4,12},{12,4},... | collective-permute-start | bytes 589832 | tf_op jit(solution)/shard_map/ppermute | solution.py:203
  20.5 12.7 %copy-start.1 = (bf16[256,256]{1,0:T(8,128)(2,1)S(1)}, bf16[256,256]{1,0:T(8,128)(2,1)}, u32[]{:S(2)}) copy-start(bf16[256,256]{1,0:T(8,128)(2,1)} %weight_ref.5) | copy-start | bytes 393220

commit v6 on v5

--- a/solution.py
+++ b/solution.py
@@ -31,6 +31,10 @@
 
 def listed(i):
     return i ^ 9
+
+
+def cam_listed(i, core):
+    return i ^ (7 - core)
 
 
 def first_stripe(camera):
@@ -162,8 +166,9 @@
     )
     total = total.astype(jnp.bfloat16)
     share = Q // CAM_DEVICES
+    core = lax.axis_index("core")
     for i in range(CAM_DEVICES):
-        out_ref[CAM_DEVICES - 1 - i] = total[i * share : (i + 1) * share, :]
+        out_ref[cam_listed(i, core)] = total[i * share : (i + 1) * share, :]
 
 
 def sample(kernel, name, out_shape, *operands):
@@ -203,13 +208,11 @@
     return lax.ppermute(x, axis, [(0, 1), (1, 0)])
 
 
-def exchanged(x, axis, order):
-    return lax.all_to_all(x, axis, 0, 0, tiled=True, axis_index_groups=[order])
-
-
 def body(features, value_weight, output_weight, hit_list, sample_index, attention, validity):
     copies = jnp.broadcast_to(features[None], (ZY_DEVICES, BLOCK, D))
-    mine = exchanged(copies, "zy", [listed(i) for i in range(ZY_DEVICES)]).reshape(ZY_DEVICES * BLOCK, D)
+    mine = lax.all_to_all(
+        copies, "zy", 0, 0, tiled=True, axis_index_groups=[[listed(i) for i in range(ZY_DEVICES)]]
+    ).reshape(ZY_DEVICES * BLOCK, D)
     mix, starts = build_mix(hit_list, sample_index.transpose(1, 2, 0), attention.T, validity.T)
     mine, mix, starts = lax.optimization_barrier((mine, mix, starts))
     other = swapped(mine, "core")
@@ -217,7 +220,12 @@
     near = sample(near_kernel, "sample_near", near_shape, starts, mine, value_weight, mix)
     pieces_shape = jax.ShapeDtypeStruct((CAM_DEVICES, Q // CAM_DEVICES, D), jnp.bfloat16)
     pieces = sample(far_kernel, "sample_far", pieces_shape, starts, other, value_weight, mix, near)
-    arrived = exchanged(pieces, "cam", list(reversed(range(CAM_DEVICES))))
+    groups = [
+        [(zy * 2 + core) * CAM_DEVICES + cam_listed(i, core) for i in range(CAM_DEVICES)]
+        for zy in range(ZY_DEVICES)
+        for core in range(2)
+    ]
+    arrived = lax.all_to_all(pieces, ("zy", "core", "cam"), 0, 0, tiled=True, axis_index_groups=groups)
     return project(arrived, output_weight)
 
 

time: 34.3 us -> 33.9 us (0.988)
  blocking collectives: 11.3 us -> 10.8 us
    all_to_all x1, blocking collectives: 11.3 us -> 10.8 us  [body(): lax.all_to_all(pieces, ('zy', 'core', 'cam'), 0, 0, tiled=True, axis_inde...]
where the time goes in v6:
time: 33.9 us; the launch traced here: 33.5 us
  blocking collectives  10.8 us (32%)
  starting transfers between devices  10.5 us (31%)
  Pallas kernels  6.88 us (20%)
  waiting for transfers between devices  3.82 us (11%)
  local copies, waits for them, and re-layouts  1.43 us (4%)
    all_to_all x1, blocking collectives, body(): lax.all_to_all(pieces, ('zy', 'core', 'cam'), 0, 0, tiled=True, axis_inde...  10.8 us
    all_to_all x1, starting transfers between devices, body(): lax.all_to_all(copies, 'zy', 0, 0, tiled=True, axis_index_groups=[[listed...  10.5 us
    pallas_call x1, Pallas kernels, build_mix(): pl.pallas_call(mix_kernel, out_shape=(jax.ShapeDtypeStruct((Q, CHUNKS * L...  4.7 us
    all_to_all x1, waiting for transfers between devices, body(): lax.all_to_all(copies, 'zy', 0, 0, tiled=True, axis_index_groups=[[listed...  3.1 us
    broadcast_in_dim x1, local copies, waits for them, and re-layouts, body(): copies = jnp.broadcast_to(features[None], (ZY_DEVICES, BLOCK, D))  1.42 us
    pallas_call x2, Pallas kernels, sample(): pl.pallas_call(kernel, out_shape=out_shape, in_specs=[whole] * len(operan...  1.4 us
    pallas_call x1, Pallas kernels, project(): pl.pallas_call(project_kernel, out_shape=jax.ShapeDtypeStruct((Q // CAM_D...  0.78 us
    ppermute x1, waiting for transfers between devices, swapped(): return lax.ppermute(x, axis, [(0, 1), (1, 0)])  0.72 us
  transfers between devices with their start and end apart: 2, of which 2 were waited for; matrix products, arithmetic and copies ran while one was open for 0% of the time, Pallas kernels for 16%

profile of v6, /device:TPU:16, one launch (start us, length us, event | category | flops | bytes accessed | tf_op | source)
XLA Modules:
  0.0 33.5 jit_solution(18057305748741515757)
XLA Ops:
  0.0 0.0 copy-start
  0.0 1.4 %broadcast_in_dim.2 = bf16[16,24,256]{2,1,0:T(8,128)(2,1)} broadcast(bf16[24,256]{1,0:T(8,128)(2,1)} %param.7), dimensions={1,2} | broadcast | bytes 208896 | tf_op jit(solution)/shard_map/broadcast_in_dim | solution.py:212
  1.4 10.5 %all-to-all-start = ((bf16[16,24,256]{2,1,0:T(8,128)(2,1)}), bf16[16,24,256]{2,1,0:T(8,128)(2,1)S(1)}, u32[]{:S(2)}, u32[]{:S(2)}) async-start(bf16[16,24,256]{2,1,0:T(8,128)(2,1)} %broadcast_in_dim.2), calls=%async_computation | async-start | bytes 393216 | tf_op jit(solution)/shard_map/all_to_all | solution.py:213
  12.0 4.7 %build_mix.1 = (bf16[512,2304]{1,0:T(8,128)(2,1)S(1)}, s32[12,128]{1,0:T(8,128)S(1)}) custom-call(s32[1,2]{1,0:T(1,128)} %hit_any.1, s32[2,64,512]{2,1,0:T(8,128)} %bitcast.6, bf16[64,512]{1,0:T(8,128)(2,1)} %bitcast.7, s32[2,512]{1,0:T(2,128)} %bitcast.8), custom_call_target="tpu_custom_call" | custom-call | flops 536870912 | bytes 4194304 | tf_op jit(solution)/shard_map/build_mix/pallas_call | solution.py:115
  16.7 3.1 %all-to-all-done = bf16[16,24,256]{2,1,0:T(8,128)(2,1)S(1)} async-done(((bf16[16,24,256]{2,1,0:T(8,128)(2,1)}), bf16[16,24,256]{2,1,0:T(8,128)(2,1)S(1)}, u32[]{:S(2)}, u32[]{:S(2)}) %all-to-all-start) | async-done | bytes 196640 | tf_op jit(solution)/shard_map/all_to_all | solution.py:213
  19.8 0.0 collective-permute-start
  19.8 0.0 copy-done
  19.8 0.7 %sample_near.1.near_ref = f32[512,256]{1,0:T(8,128)S(1)} custom-call(s32[12,128]{1,0:T(8,128)S(1)} %get-tuple-element.12.starts_ref, bf16[384,256]{1,0:T(8,128)(2,1)S(1)} %bitcast.5, bf16[256,256]{1,0:T(8,128)(2,1)S(1)} %copy-done, bf16[512,2304]{1,0:T(8,128)(2,1)S(1)} %get-tuple-element.14.mix_ref), custom_call_target="tpu_custom_call" | custom-call | flops 268435456 | bytes 1048576 | tf_op jit(solution)/shard_map/sample_near/pallas_call | solution.py:175
  20.5 0.0 copy-start.1
  20.5 0.7 %collective-permute-done.other_ref = bf16[384,256]{1,0:T(8,128)(2,1)S(1)} collective-permute-done((bf16[384,256]{1,0:T(8,128)(2,1)S(1)}, bf16[384,256]{1,0:T(8,128)(2,1)S(1)}, u32[]{:S(2)}, u32[]{:S(2)}) %collective-permute-start) | collective-permute-done | bytes 196640 | tf_op jit(solution)/shard_map/ppermute | solution.py:208
  21.2 0.7 %sample_far.1 = bf16[8,64,256]{2,1,0:T(8,128)(2,1)S(1)} custom-call(s32[12,128]{1,0:T(8,128)S(1)} %get-tuple-element.12.starts_ref, bf16[384,256]{1,0:T(8,128)(2,1)S(1)} %collective-permute-done.other_ref, bf16[256,256]{1,0:T(8,128)(2,1)S(1)} %copy-done, bf16[512,2304]{1,0:T(8,128)(2,1)S(1)} %get-tuple-element.14.mix_ref, f32[512,256]{1,0:T(8,128)S(1)} %sample_near.1.near_ref), custom_call_target="tpu_custom_call" | custom-call | flops 268435456 | bytes 1048576 | tf_op jit(solution)/shard_map/sample_far/pallas_call | solution.py:175
  21.9 10.8 %all_to_all.10.pieces_ref = bf16[8,64,256]{2,1,0:T(8,128)(2,1)S(1)} all-to-all(bf16[8,64,256]{2,1,0:T(8,128)(2,1)S(1)} %sample_far.1), channel_id=1, replica_groups={{7,6,5,4,3,2,1,0},{14,15,12,13,10,11,8,9},{23,22,21,20,19,18,17,16},{30..., dimensions={0} | all-to-all | bytes 524288 | tf_op jit(solution)/shard_map/all_to_all | solution.py:228
  32.7 0.0 copy-done.1
  32.7 0.8 %project.1 = bf16[64,256]{1,0:T(8,128)(2,1)} custom-call(bf16[8,64,256]{2,1,0:T(8,128)(2,1)S(1)} %all_to_all.10.pieces_ref, bf16[256,256]{1,0:T(8,128)(2,1)S(1)} %copy-done.1), custom_call_target="tpu_custom_call" | custom-call | tf_op jit(solution)/shard_map/project/pallas_call | solution.py:197
Async XLA Ops:
  0.0 19.8 %copy-start = (bf16[256,256]{1,0:T(8,128)(2,1)S(1)}, bf16[256,256]{1,0:T(8,128)(2,1)}, u32[]{:S(2)}) copy-start(bf16[256,256]{1,0:T(8,128)(2,1)} %weight_ref.4) | copy-start | bytes 393220
  1.4 18.4 %all-to-all-start = ((bf16[16,24,256]{2,1,0:T(8,128)(2,1)}), bf16[16,24,256]{2,1,0:T(8,128)(2,1)S(1)}, u32[]{:S(2)}, u32[]{:S(2)}) async-start(bf16[16,24,256]{2,1,0:T(8,128)(2,1)} %broadcast_in_dim.2), calls=%async_computation | async-start | bytes 393216 | tf_op jit(solution)/shard_map/all_to_all | solution.py:213
  19.8 1.4 %collective-permute-start = (bf16[384,256]{1,0:T(8,128)(2,1)S(1)}, bf16[384,256]{1,0:T(8,128)(2,1)S(1)}, u32[]{:S(2)}, u32[]{:S(2)}) collective-permute-start(bf16[384,256]{1,0:T(8,128)(2,1)S(1)} %bitcast.4), channel_id=1, source_target_pairs={{0,8},{8,0},{1,9},{9,1},{2,10},{10,2},{3,11},{11,3},{4,12},{12,4},... | collective-permute-start | bytes 589832 | tf_op jit(solution)/shard_map/ppermute | solution.py:208
  20.5 12.2 %copy-start.1 = (bf16[256,256]{1,0:T(8,128)(2,1)S(1)}, bf16[256,256]{1,0:T(8,128)(2,1)}, u32[]{:S(2)}) copy-start(bf16[256,256]{1,0:T(8,128)(2,1)} %weight_ref.5) | copy-start | bytes 393220

commit v7 on v6

--- a/solution.py
+++ b/solution.py
@@ -30,7 +30,11 @@
 
 
 def listed(i):
-    return i ^ 9
+    return ((i & 1) ^ 1) * 8 + ((i >> 1) ^ 4)
+
+
+def device_at(place):
+    return ((place & 7) ^ 4) * 2 + ((place >> 3) ^ 1)
 
 
 def cam_listed(i, core):
@@ -211,7 +215,7 @@
 def body(features, value_weight, output_weight, hit_list, sample_index, attention, validity):
     copies = jnp.broadcast_to(features[None], (ZY_DEVICES, BLOCK, D))
     mine = lax.all_to_all(
-        copies, "zy", 0, 0, tiled=True, axis_index_groups=[[listed(i) for i in range(ZY_DEVICES)]]
+        copies, "zy", 0, 0, tiled=True, axis_index_groups=[[device_at(i) for i in range(ZY_DEVICES)]]
     ).reshape(ZY_DEVICES * BLOCK, D)
     mix, starts = build_mix(hit_list, sample_index.transpose(1, 2, 0), attention.T, validity.T)
     mine, mix, starts = lax.optimization_barrier((mine, mix, starts))

time: 33.9 us -> 33.5 us (0.988)
  waiting for transfers between devices: 3.82 us -> 3.48 us
where the time goes in v7:
time: 33.5 us; the launch traced here: 33.1 us
  blocking collectives  10.8 us (32%)
  starting transfers between devices  10.5 us (31%)
  Pallas kernels  6.86 us (20%)
  waiting for transfers between devices  3.48 us (10%)
  local copies, waits for them, and re-layouts  1.43 us (4%)
    all_to_all x1, blocking collectives, body(): lax.all_to_all(pieces, ('zy', 'core', 'cam'), 0, 0, tiled=True, axis_inde...  10.8 us
    all_to_all x1, starting transfers between devices, body(): lax.all_to_all(copies, 'zy', 0, 0, tiled=True, axis_index_groups=[[device...  10.5 us
    pallas_call x1, Pallas kernels, build_mix(): pl.pallas_call(mix_kernel, out_shape=(jax.ShapeDtypeStruct((Q, CHUNKS * L...  4.68 us
    all_to_all x1, waiting for transfers between devices, body(): lax.all_to_all(copies, 'zy', 0, 0, tiled=True, axis_index_groups=[[device...  2.76 us
    broadcast_in_dim x1, local copies, waits for them, and re-layouts, body(): copies = jnp.broadcast_to(features[None], (ZY_DEVICES, BLOCK, D))  1.42 us
    pallas_call x2, Pallas kernels, sample(): pl.pallas_call(kernel, out_shape=out_shape, in_specs=[whole] * len(operan...  1.4 us
    pallas_call x1, Pallas kernels, project(): pl.pallas_call(project_kernel, out_shape=jax.ShapeDtypeStruct((Q // CAM_D...  0.78 us
    ppermute x1, waiting for transfers between devices, swapped(): return lax.ppermute(x, axis, [(0, 1), (1, 0)])  0.72 us
  transfers between devices with their start and end apart: 2, of which 2 were waited for; matrix products, arithmetic and copies ran while one was open for 0% of the time, Pallas kernels for 16%

profile of v7, /device:TPU:16, one launch (start us, length us, event | category | flops | bytes accessed | tf_op | source)
XLA Modules:
  0.0 33.1 jit_solution(16121194007291564542)
XLA Ops:
  0.0 0.0 copy-start
  0.0 1.4 %broadcast_in_dim.2 = bf16[16,24,256]{2,1,0:T(8,128)(2,1)} broadcast(bf16[24,256]{1,0:T(8,128)(2,1)} %param.7), dimensions={1,2} | broadcast | bytes 208896 | tf_op jit(solution)/shard_map/broadcast_in_dim | solution.py:216
  1.4 10.5 %all-to-all-start = ((bf16[16,24,256]{2,1,0:T(8,128)(2,1)}), bf16[16,24,256]{2,1,0:T(8,128)(2,1)S(1)}, u32[]{:S(2)}, u32[]{:S(2)}) async-start(bf16[16,24,256]{2,1,0:T(8,128)(2,1)} %broadcast_in_dim.2), calls=%async_computation | async-start | bytes 393216 | tf_op jit(solution)/shard_map/all_to_all | solution.py:217
  11.9 4.7 %build_mix.1 = (bf16[512,2304]{1,0:T(8,128)(2,1)S(1)}, s32[12,128]{1,0:T(8,128)S(1)}) custom-call(s32[1,2]{1,0:T(1,128)} %hit_any.1, s32[2,64,512]{2,1,0:T(8,128)} %bitcast.6, bf16[64,512]{1,0:T(8,128)(2,1)} %bitcast.7, s32[2,512]{1,0:T(2,128)} %bitcast.8), custom_call_target="tpu_custom_call" | custom-call | flops 536870912 | bytes 4194304 | tf_op jit(solution)/shard_map/build_mix/pallas_call | solution.py:119
  16.6 2.8 %all-to-all-done = bf16[16,24,256]{2,1,0:T(8,128)(2,1)S(1)} async-done(((bf16[16,24,256]{2,1,0:T(8,128)(2,1)}), bf16[16,24,256]{2,1,0:T(8,128)(2,1)S(1)}, u32[]{:S(2)}, u32[]{:S(2)}) %all-to-all-start) | async-done | bytes 196640 | tf_op jit(solution)/shard_map/all_to_all | solution.py:217
  19.4 0.0 collective-permute-start
  19.4 0.0 copy-done
  19.4 0.7 %sample_near.1.near_ref = f32[512,256]{1,0:T(8,128)S(1)} custom-call(s32[12,128]{1,0:T(8,128)S(1)} %get-tuple-element.12.starts_ref, bf16[384,256]{1,0:T(8,128)(2,1)S(1)} %bitcast.5, bf16[256,256]{1,0:T(8,128)(2,1)S(1)} %copy-done, bf16[512,2304]{1,0:T(8,128)(2,1)S(1)} %get-tuple-element.14.mix_ref), custom_call_target="tpu_custom_call" | custom-call | flops 268435456 | bytes 1048576 | tf_op jit(solution)/shard_map/sample_near/pallas_call | solution.py:179
  20.1 0.0 copy-start.1
  20.1 0.7 %collective-permute-done.other_ref = bf16[384,256]{1,0:T(8,128)(2,1)S(1)} collective-permute-done((bf16[384,256]{1,0:T(8,128)(2,1)S(1)}, bf16[384,256]{1,0:T(8,128)(2,1)S(1)}, u32[]{:S(2)}, u32[]{:S(2)}) %collective-permute-start) | collective-permute-done | bytes 196640 | tf_op jit(solution)/shard_map/ppermute | solution.py:212
  20.8 0.7 %sample_far.1 = bf16[8,64,256]{2,1,0:T(8,128)(2,1)S(1)} custom-call(s32[12,128]{1,0:T(8,128)S(1)} %get-tuple-element.12.starts_ref, bf16[384,256]{1,0:T(8,128)(2,1)S(1)} %collective-permute-done.other_ref, bf16[256,256]{1,0:T(8,128)(2,1)S(1)} %copy-done, bf16[512,2304]{1,0:T(8,128)(2,1)S(1)} %get-tuple-element.14.mix_ref, f32[512,256]{1,0:T(8,128)S(1)} %sample_near.1.near_ref), custom_call_target="tpu_custom_call" | custom-call | flops 268435456 | bytes 1048576 | tf_op jit(solution)/shard_map/sample_far/pallas_call | solution.py:179
  21.5 10.8 %all_to_all.10.pieces_ref = bf16[8,64,256]{2,1,0:T(8,128)(2,1)S(1)} all-to-all(bf16[8,64,256]{2,1,0:T(8,128)(2,1)S(1)} %sample_far.1), channel_id=1, replica_groups={{7,6,5,4,3,2,1,0},{14,15,12,13,10,11,8,9},{23,22,21,20,19,18,17,16},{30..., dimensions={0} | all-to-all | bytes 524288 | tf_op jit(solution)/shard_map/all_to_all | solution.py:232
  32.3 0.0 copy-done.1
  32.3 0.8 %project.1 = bf16[64,256]{1,0:T(8,128)(2,1)} custom-call(bf16[8,64,256]{2,1,0:T(8,128)(2,1)S(1)} %all_to_all.10.pieces_ref, bf16[256,256]{1,0:T(8,128)(2,1)S(1)} %copy-done.1), custom_call_target="tpu_custom_call" | custom-call | tf_op jit(solution)/shard_map/project/pallas_call | solution.py:201
Async XLA Ops:
  0.0 19.4 %copy-start = (bf16[256,256]{1,0:T(8,128)(2,1)S(1)}, bf16[256,256]{1,0:T(8,128)(2,1)}, u32[]{:S(2)}) copy-start(bf16[256,256]{1,0:T(8,128)(2,1)} %weight_ref.4) | copy-start | bytes 393220
  1.4 18.0 %all-to-all-start = ((bf16[16,24,256]{2,1,0:T(8,128)(2,1)}), bf16[16,24,256]{2,1,0:T(8,128)(2,1)S(1)}, u32[]{:S(2)}, u32[]{:S(2)}) async-start(bf16[16,24,256]{2,1,0:T(8,128)(2,1)} %broadcast_in_dim.2), calls=%async_computation | async-start | bytes 393216 | tf_op jit(solution)/shard_map/all_to_all | solution.py:217
  19.4 1.4 %collective-permute-start = (bf16[384,256]{1,0:T(8,128)(2,1)S(1)}, bf16[384,256]{1,0:T(8,128)(2,1)S(1)}, u32[]{:S(2)}, u32[]{:S(2)}) collective-permute-start(bf16[384,256]{1,0:T(8,128)(2,1)S(1)} %bitcast.4), channel_id=1, source_target_pairs={{0,8},{8,0},{1,9},{9,1},{2,10},{10,2},{3,11},{11,3},{4,12},{12,4},... | collective-permute-start | bytes 589832 | tf_op jit(solution)/shard_map/ppermute | solution.py:212
  20.1 12.2 %copy-start.1 = (bf16[256,256]{1,0:T(8,128)(2,1)S(1)}, bf16[256,256]{1,0:T(8,128)(2,1)}, u32[]{:S(2)}) copy-start(bf16[256,256]{1,0:T(8,128)(2,1)} %weight_ref.5) | copy-start | bytes 393220
